TPU v7x, 32 devices: a whole 2x2x4 slice. The times are simulated.
32 devices in a mesh: leaf: 2 (over y), user: 4 (over x, core), tensor: 4 (over z).
Axes of the slice: x: 2, y: 2, z: 4, core: 2. Of those that a mesh axis runs over, the one named last changes fastest.
Arguments:
- user_feat: bfloat16 [32, 128], P('user'), may hold values from -6 to 6
- beam_nodes: int32 [32, 128], P('user', ('leaf', 'tensor')), may hold values from 0 to 16383, as said below
- item_ids: int32 [32, 384], P('user', 'leaf'), may hold values from 0 to 16383, as said below
- subtree_slot: int32 [32], replicated, may hold values from 0 to 31, as said below
- node_table: bfloat16 [16384, 128], P(('leaf', 'tensor')), may hold values from -6 to 6
- item_table: bfloat16 [16384, 128], P(('leaf', 'tensor')), may hold values from -6 to 6
- mlp_user: bfloat16 [128, 1024], replicated, may hold values from -0.375 to 0.375
- mlp_node: bfloat16 [128, 1024], replicated, may hold values from -0.375 to 0.375
- mlp_bias: float32 [1024], replicated, may hold values from -3 to 3
- mlp_out: bfloat16 [1024], replicated, may hold values from -0.1875 to 0.1875
- proj_in: bfloat16 [384, 2048], P(None, 'tensor'), may hold values from -0.3125 to 0.3125
- cross_w: bfloat16 [2, 2048, 2048], P(None, None, 'tensor'), may hold values from -0.125 to 0.125
- cross_b: float32 [2, 2048], P(None, 'tensor'), may hold values from -3 to 3
- out_w: bfloat16 [2048], P('tensor'), may hold values from -0.125 to 0.125
Outputs:
- beam_score: float32 [32, 128], P('user', ('leaf', 'tensor'))
- interest: float32 [32, 128], P('user')
- logit: float32 [32, 384], P('user', 'leaf')
Inputs may be any that keep to these rules, and one draw needn't show every extreme that they name: A permutation of the subtrees: subtree s is held by index subtree_slot[s] // 4 of leaf+tensor (leaf-major), as its block subtree_slot[s] % 4. `beam_nodes`: within the 8 x 16 block of one device, at most 16 nodes belong to subtrees held by any one index of leaf+tensor; some index receives exactly 16 from every device's block. `item_ids`: split a device's 8 x 192 block, flattened user by user, into 4 runs of 384 items; each run has at most 48 items of subtrees held by any one index of leaf+tensor, and some index receives exactly 48 from every run.
All inputs are finite; a program needn't handle non-finite values.
Results may differ from a plain program's by a relative error of at most 0.0062.
Values may be sent and summed in bfloat16 or wider, within the bound.
A program may use at most 64 MiB of HBM per device.

v0:
```python
import math

import jax
import jax.numpy as jnp
from jax import lax
from jax.sharding import PartitionSpec as P

LAYERS = 2
SUB_NODES = 512
SUB_ITEMS = 512


def small_lookup(table, index):
    hits = index[:, None] == jnp.arange(table.shape[0], dtype=jnp.int32)[None, :]
    return jnp.sum(jnp.where(hits, table[None, :], 0), axis=1)


def bucket_slots(owner, owners, capacity):
    marks = (owner[:, None] == jnp.arange(owners, dtype=jnp.int32)[None, :]).astype(jnp.int32)
    before = jnp.cumsum(marks, axis=0) - marks
    rank = jnp.sum(before * marks, axis=1)
    return owner * capacity + rank


def place_ids(values, dest, total):
    return jnp.full((total,), -1, jnp.int32).at[dest].set(values)


def table_rows(table, wanted):
    found = table[jnp.clip(wanted, 0, None)]
    return jnp.where((wanted >= 0)[..., None], found, jnp.zeros_like(found))


def node_scores(user_rows, node_rows, mlp_node, mlp_bias, mlp_out):
    pre = user_rows + jnp.dot(node_rows, mlp_node, preferred_element_type=jnp.float32) + mlp_bias
    hidden = jax.nn.silu(pre).astype(jnp.bfloat16)
    return jnp.dot(hidden, mlp_out, preferred_element_type=jnp.float32)


def fetch_items(wanted_ids, capacity, owners, subtree_slot, item_table):
    sub_count = item_table.shape[0] // SUB_ITEMS
    slot = small_lookup(subtree_slot, wanted_ids // SUB_ITEMS)
    owner = slot // sub_count
    local = slot % sub_count * SUB_ITEMS + wanted_ids % SUB_ITEMS
    dest = bucket_slots(owner, owners, capacity)
    send = place_ids(local, dest, owners * capacity).reshape(owners, capacity)
    arrived = lax.all_to_all(
        table_rows(
            item_table,
            lax.all_to_all(send, ("leaf", "tensor"), split_axis=0, concat_axis=0, tiled=True),
        ),
        ("leaf", "tensor"),
        split_axis=0,
        concat_axis=0,
        tiled=True,
    )
    return arrived.reshape(owners * capacity, -1)[dest]


def per_device(
    user_feat,
    beam_nodes,
    item_ids,
    subtree_slot,
    node_table,
    item_table,
    mlp_user,
    mlp_node,
    mlp_bias,
    mlp_out,
    proj_in,
    cross_w,
    cross_b,
    out_w,
):
    leaf_count = lax.axis_size("leaf")
    tensor_count = lax.axis_size("tensor")
    owners = leaf_count * tensor_count
    users_here, beam_here = beam_nodes.shape
    requests = users_here * beam_here
    beam_cap = max(2, -(-requests // owners))
    sub_count = node_table.shape[0] // SUB_NODES
    flat_nodes = beam_nodes.reshape(-1)
    node_slot = small_lookup(subtree_slot, flat_nodes // SUB_NODES)
    node_owner = node_slot // sub_count
    node_local = node_slot % sub_count * SUB_NODES + flat_nodes % SUB_NODES
    node_dest = bucket_slots(node_owner, owners, beam_cap)
    node_send = place_ids(node_local, node_dest, owners * beam_cap).reshape(owners, beam_cap)
    user_part = jnp.dot(user_feat, mlp_user, preferred_element_type=jnp.float32)
    request_user = jnp.arange(requests, dtype=jnp.int32) // beam_here
    arrived = lax.all_to_all(
        table_rows(
            node_table,
            lax.all_to_all(node_send, ("leaf", "tensor"), split_axis=0, concat_axis=0, tiled=True),
        ),
        ("leaf", "tensor"),
        split_axis=0,
        concat_axis=0,
        tiled=True,
    )
    node_rows = arrived.reshape(owners * beam_cap, -1)[node_dest]
    scores = node_scores(user_part[request_user], node_rows, mlp_node, mlp_bias, mlp_out)
    weighted = jax.nn.sigmoid(scores)[:, None] * node_rows.astype(jnp.float32)
    numerator = jnp.sum(weighted.reshape(users_here, beam_here, -1), axis=1)
    interest_total = lax.psum(numerator, ("leaf", "tensor"))
    interest = interest_total / math.sqrt(owners * beam_here)
    beam_score = scores.reshape(users_here, beam_here)
    items_here = item_ids.shape[1]
    rows = users_here * items_here
    fetch = rows // tensor_count
    item_cap = max(2, -(-fetch // owners))
    flat_items = item_ids.reshape(-1)
    start = lax.axis_index("tensor") * fetch
    rotated = jnp.roll(flat_items, -start)
    rotated_rows = fetch_items(rotated, tensor_count * item_cap, owners, subtree_slot, item_table)
    item_vec = jnp.roll(rotated_rows, start, axis=0)
    interest_b = interest.astype(jnp.bfloat16)
    user_cols = jnp.repeat(user_feat, items_here, axis=0)
    interest_cols = jnp.repeat(interest_b, items_here, axis=0)
    inputs = jnp.concatenate([user_cols, interest_cols, item_vec], axis=1)
    x_first = jnp.dot(inputs, proj_in, preferred_element_type=jnp.float32).astype(jnp.bfloat16)
    first_wide = x_first.astype(jnp.float32)
    x_now = x_first
    for layer in range(LAYERS):
        weight = cross_w[layer]
        mixed = jnp.dot(
            lax.all_gather(x_now, "tensor", axis=1, tiled=True),
            weight,
            preferred_element_type=jnp.float32,
        )
        x_now = (first_wide * (mixed + cross_b[layer]) + x_now.astype(jnp.float32)).astype(
            jnp.bfloat16
        )
    partial_logit = jnp.dot(x_now, out_w, preferred_element_type=jnp.float32)
    logit = lax.psum(partial_logit, "tensor").reshape(users_here, items_here)
    return (beam_score, interest, logit)


def solution(mesh):
    placed = (
        P("user", None),
        P("user", ("leaf", "tensor")),
        P("user", "leaf"),
        P(),
        P(("leaf", "tensor"), None),
        P(("leaf", "tensor"), None),
        P(),
        P(),
        P(),
        P(),
        P(None, "tensor"),
        P(None, None, "tensor"),
        P(None, "tensor"),
        P("tensor"),
    )
    return jax.shard_map(
        per_device,
        mesh=mesh,
        in_specs=placed,
        out_specs=(P("user", ("leaf", "tensor")), P("user", None), P("user", "leaf")),
        check_vma=False,
    )
```

profile of v0, /device:TPU:0, one launch (start us, length us, event | category | flops | bytes accessed | tf_op | source)
XLA Modules:
  0.0 349.3 jit_solution(13803340638671157353)
XLA Ops:
  7.2 0.0 copy-start
  7.2 0.9 reshape.317
  8.1 0.7 select_reduce_fusion.2
  8.8 0.1 fusion.23
  8.9 0.2 reduce_window_sum.26
  9.1 0.2 select_reduce_fusion.1
  9.3 1.0 scatter_custom_fusion
  10.3 0.7 all_to_all.18
  10.9 7.3 %all-to-all-start = ((s32[8,1,16]{2,1,0:T(1,128)}), s32[8,1,16]{2,1,0:T(1,128)S(1)}, u32[]{:S(2)}, u32[]{:S(2)}) async-start(s32[8,1,16]{2,1,0:T(1,128)} %bitcast.4), calls=%async_computation | async-start | bytes 8192 | tf_op jit(solution)/shard_map/all_to_all | solution.py:94
  18.2 0.8 reshape.322
  19.0 0.1 add_select_fusion.4
  19.1 0.8 select_reduce_fusion
  19.9 0.1 fusion.30
  20.0 2.3 reduce-window.6
  22.3 0.3 slice_reduce_fusion
  22.6 0.2 reduce-window.9
  22.8 0.1 add_bitcast_fusion
  22.9 0.1 fusion.36
  23.0 1.1 fusion.51
  24.1 6.2 %scatter_custom_fusion.1 = s32[1536]{0:T(1024)S(1)} fusion(s32[1536]{0:T(1024)S(1)} %fusion.36, s32[1536]{0:T(1024)S(1)} %get-tuple-element.5, s32[]{:T(128)} %constant.148.clone.1), kind=kCustom, calls=%fused_computation.98 | custom fusion | bytes 6148 | tf_op jit(solution)/shard_map/scatter | solution.py:26
  30.3 0.7 all_to_all.21
  31.0 0.7 reshape.387
  31.7 0.8 gather_fusion
  32.5 0.0 copy-start.7
  32.5 0.0 copy-start.8
  32.5 0.0 all-to-all-done
  32.5 6.1 %all-to-all-start.2 = ((s32[8,1,192]{2,1,0:T(1,128)}), s32[8,1,192]{2,1,0:T(1,128)S(1)}, u32[]{:S(2)}, u32[]{:S(2)}) async-start(s32[8,1,192]{2,1,0:T(1,128)} %all_to_all.21), calls=%async_computation.2 | async-start | bytes 16384 | tf_op jit(solution)/shard_map/all_to_all | solution.py:50
  38.7 0.1 reshape.337
  38.7 0.7 gather_fusion.1
  39.5 0.7 broadcast_select_fusion.1
  40.2 5.0 %all-to-all-done.2 = s32[8,1,192]{2,1,0:T(1,128)S(1)} async-done(((s32[8,1,192]{2,1,0:T(1,128)}), s32[8,1,192]{2,1,0:T(1,128)S(1)}, u32[]{:S(2)}, u32[]{:S(2)}) %all-to-all-start.2) | async-done | bytes 6176 | tf_op jit(solution)/shard_map/all_to_all | solution.py:50
  45.2 3.3 all-to-all-start.1
  48.5 0.1 reshape.353
  48.6 0.0 copy-done
  48.6 3.2 gather_fusion.3
  51.8 1.0 broadcast_select_fusion
  52.8 2.3 all-to-all-done.1
  55.2 3.6 %all-to-all-start.3 = ((bf16[8,192,128]{2,1,0:T(8,128)(2,1)}), bf16[8,192,128]{2,1,0:T(8,128)(2,1)S(1)}, u32[]{:S(2)}, u32[]{:S(2)}) async-start(bf16[8,192,128]{2,1,0:T(8,128)(2,1)} %broadcast_select_fusion), calls=%async_computation.3 | async-start | bytes 786432 | tf_op jit(solution)/shard_map/all_to_all | solution.py:47
  58.8 0.0 all-gather.3.cloned.1.call-start
  58.8 0.7 gather_fusion.2
  59.5 0.0 copy-done.7
  59.6 0.0 copy-start.3
  59.6 0.4 add_divide_fusion
  59.9 0.1 mul.66
  60.1 0.1 fusion.22
  60.2 21.9 %psum.14 = f32[8,128]{1,0:T(8,128)S(1)} all-reduce(f32[8,128]{1,0:T(8,128)S(1)} %fusion.22), channel_id=1, replica_groups=mesh['leaf'=2,'user'=4,'tensor'=4] {'leaf','tensor'}, use_global_device_ids=true, to_apply=%region_5.6 | all-reduce | flops 1024 | bytes 8192 | tf_op jit(solution)/shard_map/psum | solution.py:105
  82.1 0.6 fusion.49
  82.7 0.0 all-to-all-done.3
  82.7 3.2 gather_fusion.4
  85.9 1.5 fusion.19
  87.4 0.1 broadcast_in_dim.85
  87.5 0.1 broadcast_in_dim.84
  87.5 0.0 copy-start.4
  87.6 2.1 convolution_convert_fusion
  89.7 0.0 all-gather.3.cloned.1.call-update
  89.7 0.2 all-gather.5.cloned.1.call-start
  90.0 112.5 %all-gather.3.cloned.1.call-done = bf16[1536,2048]{1,0:T(8,128)(2,1)} async-done(((bf16[1536,512]{1,0:T(8,128)(2,1)}), bf16[1536,2048]{1,0:T(8,128)(2,1)}) %all-gather.3.cloned.1.call-update) | async-done | bytes 6291472 | tf_op jit(solution)/shard_map/all_gather | solution.py:127
  202.4 8.8 %fusion.1 = bf16[1536,512]{1,0:T(8,128)(2,1)} fusion(bf16[1536,512]{1,0:T(8,128)(2,1)} %convolution_convert_fusion, bf16[1536,2048]{1,0:T(8,128)(2,1)} %all-gather.3.cloned.1.call-done, bf16[2,2048,512]{2,1,0:T(8,128)(2,1)} %param.25, f32[512]{0:T(512)S(1)} %bitcast.106), kind=kOutput, calls=%fused_computation.12 | convolution fusion | flops 3225157632 | bytes 11536384 | tf_op jit(solution)/shard_map/dot_general | solution.py:126
  211.3 0.0 all-gather.5.cloned.1.call-update
  211.3 0.7 reshape.319
  212.0 113.0 %all-gather.5.cloned.1.call-done = bf16[1536,2048]{1,0:T(8,128)(2,1)} async-done(((bf16[1536,512]{1,0:T(8,128)(2,1)}), bf16[1536,2048]{1,0:T(8,128)(2,1)}) %all-gather.5.cloned.1.call-update) | async-done | bytes 6291472 | tf_op jit(solution)/shard_map/all_gather | solution.py:127
  325.0 8.0 %fusion.16 = f32[1536]{0:T(1024)S(1)} fusion(bf16[512,1]{0,1:T(2,128)(2,1)S(1)} %reshape.389, bf16[1536,512]{1,0:T(8,128)(2,1)} %fusion.1, bf16[1536,2048]{1,0:T(8,128)(2,1)} %all-gather.5.cloned.1.call-done, bf16[1536,512]{1,0:T(8,128)(2,1)S(1)} %copy-done.1, bf16[2,2048,512]{2,1,0:T(8,128)(2,1)} %param.25, f32[512]{0:T(512)S(1)} %bitcast.105), kind=kOutput, calls=%fused_computation.27 | convolution fusion | flops 3227516928 | bytes 11543552 | tf_op jit(solution)/shard_map/dot_general | solution.py:134
  333.0 0.1 reshape.325
  333.1 9.4 %psum.15 = f32[8,192]{1,0:T(8,128)} all-reduce(f32[8,192]{1,0:T(8,128)S(1)} %reshape.325), channel_id=1, replica_groups=mesh['leaf'=2,'user'=4,'tensor'=4] {'tensor'}, use_global_device_ids=true, to_apply=%region_11.12 | all-reduce | flops 1536 | bytes 12288 | tf_op jit(solution)/shard_map/psum | solution.py:135
  (28 shorter events, 0.2 us)
Async XLA Ops:
  7.2 41.4 %copy-start = (bf16[2048,128]{1,0:T(8,128)(2,1)S(1)}, bf16[2048,128]{1,0:T(8,128)(2,1)}, u32[]{:S(2)}) copy-start(bf16[2048,128]{1,0:T(8,128)(2,1)} %param.19) | copy-start | bytes 1572868
  7.2 31.6 %copy-start.2 = (bf16[2048,128]{1,0:T(8,128)(2,1)S(1)}, bf16[2048,128]{1,0:T(8,128)(2,1)}, u32[]{:S(2)}) copy-start(bf16[2048,128]{1,0:T(8,128)(2,1)} %param.18) | copy-start | bytes 1572868
  10.9 21.5 %all-to-all-start = ((s32[8,1,16]{2,1,0:T(1,128)}), s32[8,1,16]{2,1,0:T(1,128)S(1)}, u32[]{:S(2)}, u32[]{:S(2)}) async-start(s32[8,1,16]{2,1,0:T(1,128)} %bitcast.4), calls=%async_computation | async-start | bytes 8192 | tf_op jit(solution)/shard_map/all_to_all | solution.py:94
  32.5 27.1 %copy-start.7 = (bf16[128,1024]{1,0:T(8,128)(2,1)S(1)}, bf16[128,1024]{1,0:T(8,128)(2,1)}, u32[]{:S(2)}) copy-start(bf16[128,1024]{1,0:T(8,128)(2,1)} %param.21) | copy-start | bytes 786436
  32.5 27.1 %copy-start.8 = (f32[1024]{0:T(1024)S(1)}, f32[1024]{0:T(1024)}, u32[]{:S(2)}) copy-start(f32[1024]{0:T(1024)} %param.22) | copy-start | bytes 12292
  32.5 12.7 %all-to-all-start.2 = ((s32[8,1,192]{2,1,0:T(1,128)}), s32[8,1,192]{2,1,0:T(1,128)S(1)}, u32[]{:S(2)}, u32[]{:S(2)}) async-start(s32[8,1,192]{2,1,0:T(1,128)} %all_to_all.21), calls=%async_computation.2 | async-start | bytes 16384 | tf_op jit(solution)/shard_map/all_to_all | solution.py:50
  45.2 10.0 %all-to-all-start.1 = ((bf16[8,16,128]{2,1,0:T(8,128)(2,1)}), bf16[8,16,128]{2,1,0:T(8,128)(2,1)S(1)}, u32[]{:S(2)}, u32[]{:S(2)}) async-start(bf16[8,16,128]{2,1,0:T(8,128)(2,1)} %broadcast_select_fusion.1), calls=%async_computation.1 | async-start | bytes 65536 | tf_op jit(solution)/shard_map/all_to_all | solution.py:91
  55.2 27.5 %all-to-all-start.3 = ((bf16[8,192,128]{2,1,0:T(8,128)(2,1)}), bf16[8,192,128]{2,1,0:T(8,128)(2,1)S(1)}, u32[]{:S(2)}, u32[]{:S(2)}) async-start(bf16[8,192,128]{2,1,0:T(8,128)(2,1)} %broadcast_select_fusion), calls=%async_computation.3 | async-start | bytes 786432 | tf_op jit(solution)/shard_map/all_to_all | solution.py:47
  58.8 143.7 %all-gather.3.cloned.1.call-start = ((), (), s32[]{:S(2)}) async-start(), calls=%async_computation.4 | async-start | bytes 7864320 | tf_op jit(solution)/shard_map/all_gather | solution.py:127
  59.6 27.9 %copy-start.3 = (bf16[8,128]{1,0:T(8,128)(2,1)S(1)}, bf16[8,128]{1,0:T(8,128)(2,1)}, u32[]{:S(2)}) copy-start(bf16[8,128]{1,0:T(8,128)(2,1)} %param.14) | copy-start | bytes 6148
  59.9 27.6 %copy-start.6 = (bf16[384,512]{1,0:T(8,128)(2,1)S(1)}, bf16[384,512]{1,0:T(8,128)(2,1)}, u32[]{:S(2)}) copy-start(bf16[384,512]{1,0:T(8,128)(2,1)} %param.24) | copy-start | bytes 1179652
  87.5 2.4 copy-start.4
  89.7 235.3 %all-gather.5.cloned.1.call-start = ((), (), s32[]{:S(2)}) async-start(), calls=%async_computation.5 | async-start | bytes 7864320 | tf_op jit(solution)/shard_map/all_gather | solution.py:127
  202.4 8.9 %copy-start.5 = (bf16[512]{0:T(512)(128)(2,1)S(1)}, bf16[512]{0:T(512)(128)(2,1)}, u32[]{:S(2)}) copy-start(bf16[512]{0:T(512)(128)(2,1)} %param.27) | copy-start | bytes 3076
  202.4 122.5 %copy-start.1 = (bf16[1536,512]{1,0:T(8,128)(2,1)S(1)}, bf16[1536,512]{1,0:T(8,128)(2,1)}, u32[]{:S(2)}) copy-start(bf16[1536,512]{1,0:T(8,128)(2,1)} %convolution_convert_fusion) | copy-start | bytes 4718596
Sparse Core Ops, SparseCore 0:
  89.8 112.5 all-gather.2
  211.4 113.4 all-gather.4
where the time goes:
time: 350 us; the launch traced here: 349 us
  waiting for transfers between devices  233 us (67%)
  blocking collectives  31.2 us (9%)
  local copies, waits for them, and re-layouts  20.9 us (6%)
  starting transfers between devices  20.6 us (6%)
  matrix products  20.5 us (6%)
  between operations  14.4 us (4%)
  other arithmetic  8.75 us (2%)
    all_gather x2, waiting for transfers between devices, per_device(): lax.all_gather(x_now, 'tensor', axis=1, tiled=True)  225 us
    psum x1, blocking collectives, per_device(): interest_total = lax.psum(numerator, ('leaf', 'tensor'))  21.9 us
    psum x1, blocking collectives, per_device(): logit = lax.psum(partial_logit, 'tensor').reshape(users_here, items_here)  9.35 us
    dot_general x1, matrix products, per_device(): jnp.dot(lax.all_gather(x_now, 'tensor', axis=1, tiled=True), weight, pref...  8.83 us
    dot_general x1, matrix products, per_device(): partial_logit = jnp.dot(x_now, out_w, preferred_element_type=jnp.float32)  8.02 us
    all_to_all x1, starting transfers between devices, per_device(): lax.all_to_all(node_send, ('leaf', 'tensor'), split_axis=0, concat_axis=0...  7.31 us
    scatter x2, local copies, waits for them, and re-layouts, place_ids(): return jnp.full((total,), -1, jnp.int32).at[dest].set(values)  7.16 us
  transfers between devices with their start and end apart: 6, of which 4 were waited for; matrix products, arithmetic and copies ran while one was open for 6% of the time, Pallas kernels for 0%

commit v1 on v0

v1 whole, which is shorter than its diff:
```python
import math

import jax
import jax.numpy as jnp
from jax import lax
from jax.sharding import PartitionSpec as P

SUB_NODES = 512
SUB_ITEMS = 512
BOTH = ("leaf", "tensor")
F32 = jnp.float32
BF16 = jnp.bfloat16


def small_lookup(table, index):
    hits = index[..., None] == jnp.arange(table.shape[0], dtype=jnp.int32)
    return jnp.sum(jnp.where(hits, table, 0), axis=-1)


def locate(ids, span, subtree_slot, rows):
    slot = small_lookup(subtree_slot, ids // span)
    per = rows // span
    return slot // per, slot % per * span + ids % span


def rank_in_row(marks):
    n = marks.shape[-1]
    at = jnp.arange(n, dtype=jnp.int32)
    before = (at[:, None] < at[None, :]).astype(BF16)
    return jnp.dot(marks.astype(BF16), before, preferred_element_type=F32).astype(jnp.int32)


def pick_rows(table, wanted):
    hot = (wanted[:, None] == jnp.arange(table.shape[0], dtype=jnp.int32)[None, :]).astype(BF16)
    return jnp.dot(hot, table, preferred_element_type=F32).astype(BF16)


def owned_slots(owner, local, me, cap):
    mine = owner == me
    rank = rank_in_row(mine)
    chosen = mine[:, None, :] & (
        rank[:, None, :] == jnp.arange(cap, dtype=jnp.int32)[None, :, None]
    )
    wanted = jnp.sum(jnp.where(chosen, local[:, None, :] + 1, 0), axis=2) - 1
    return chosen, wanted


def per_device(
    user_feat,
    beam_nodes,
    item_ids,
    subtree_slot,
    node_table,
    item_table,
    mlp_user,
    mlp_node,
    mlp_bias,
    mlp_out,
    proj_in,
    cross_w,
    cross_b,
    out_w,
):
    leafs = lax.axis_size("leaf")
    tensors = lax.axis_size("tensor")
    owners = leafs * tensors
    tensor_at = lax.axis_index("tensor")
    me = lax.axis_index("leaf") * tensors + tensor_at
    users, beam = beam_nodes.shape
    items = item_ids.shape[1]
    width = user_feat.shape[1]

    proj_all = lax.all_gather(proj_in, "tensor", axis=1, tiled=True)
    first_here = jnp.dot(proj_all, cross_w[0], preferred_element_type=F32).astype(BF16)
    first_all = lax.all_gather(first_here, "tensor", axis=1, tiled=True)
    bias_all = lax.all_gather(cross_b[0], "tensor", axis=0, tiled=True)

    requests = users * beam
    cap_b = max(2, -(-requests // owners))
    node_ids = lax.all_gather(beam_nodes.reshape(-1), BOTH, axis=0)
    n_owner, n_local = locate(node_ids, SUB_NODES, subtree_slot, node_table.shape[0])
    n_chosen, n_wanted = owned_slots(n_owner, n_local, me, cap_b)
    asker = jnp.arange(requests, dtype=jnp.int32) // beam
    n_user = jnp.sum(jnp.where(n_chosen, asker[None, None, :], 0), axis=2).reshape(-1)
    node_rows = pick_rows(node_table, n_wanted.reshape(-1))
    user_hot = n_user[:, None] == jnp.arange(users, dtype=jnp.int32)[None, :]
    user_rows = jnp.dot(user_hot.astype(BF16), user_feat, preferred_element_type=F32).astype(BF16)
    pre = (
        jnp.dot(user_rows, mlp_user, preferred_element_type=F32)
        + jnp.dot(node_rows, mlp_node, preferred_element_type=F32)
        + mlp_bias
    )
    hidden = jax.nn.silu(pre).astype(BF16)
    scores = jnp.dot(hidden, mlp_out, preferred_element_type=F32)
    held = n_wanted.reshape(-1) >= 0
    gate = jnp.where(user_hot & held[:, None], jax.nn.sigmoid(scores)[:, None], 0.0)
    numerator = lax.dot_general(
        gate, node_rows.astype(F32), (((0,), (0,)), ((), ())), precision=lax.Precision.HIGHEST
    )
    back = jnp.sum(jnp.where(n_chosen, scores.reshape(owners, cap_b, 1), 0.0), axis=1)
    summed = lax.psum(jnp.concatenate([numerator.reshape(-1), back.reshape(-1)]), BOTH)
    interest = summed[: users * width].reshape(users, width) / math.sqrt(owners * beam)
    beam_score = lax.dynamic_slice(
        summed, (users * width + me * requests,), (requests,)
    ).reshape(users, beam)

    rows = users * items
    fetch = rows // tensors
    cap_i = max(2, -(-fetch // owners))
    item_all = lax.all_gather(item_ids.reshape(-1), "leaf", axis=0).reshape(owners, fetch)
    i_owner, i_local = locate(item_all, SUB_ITEMS, subtree_slot, item_table.shape[0])
    _, i_wanted = owned_slots(i_owner, i_local, me, cap_i)
    sent = pick_rows(item_table, i_wanted.reshape(-1)).reshape(owners, cap_i, width)
    arrived = lax.all_to_all(sent, BOTH, split_axis=0, concat_axis=0, tiled=True)
    my_owner = lax.dynamic_slice(i_owner, (me, 0), (1, fetch))[0]
    marks = my_owner[None, :] == jnp.arange(owners, dtype=jnp.int32)[:, None]
    place = jnp.sum(jnp.where(marks, rank_in_row(marks), 0), axis=0) + my_owner * cap_i
    run_rows = pick_rows(arrived.reshape(owners * cap_i, width), place)
    item_rows = lax.all_gather(run_rows, "tensor", axis=0, tiled=True)

    shared = jnp.concatenate([user_feat, interest.astype(BF16)], axis=1)
    two = 2 * width
    base0 = jnp.dot(shared, proj_all[:two], preferred_element_type=F32)
    base1 = jnp.dot(shared, first_all[:two], preferred_element_type=F32) + bias_all
    x0 = jnp.dot(item_rows, proj_all[two:], preferred_element_type=F32).reshape(users, items, -1)
    mixed = jnp.dot(item_rows, first_all[two:], preferred_element_type=F32).reshape(users, items, -1)
    x0 = x0 + base0[:, None, :]
    mixed = mixed + base1[:, None, :]
    x1 = (x0 * mixed + x0).astype(BF16).reshape(rows, -1)
    second = jnp.dot(x1, cross_w[1], preferred_element_type=F32)
    cols = proj_in.shape[1]
    x0_here = lax.dynamic_slice(x0.astype(BF16).reshape(rows, -1), (0, tensor_at * cols), (rows, cols))
    x1_here = lax.dynamic_slice(x1, (0, tensor_at * cols), (rows, cols))
    x2 = x0_here.astype(F32) * (second + cross_b[1]) + x1_here.astype(F32)
    partial = jnp.sum(x2 * out_w.astype(F32), axis=1)
    logit = lax.psum(partial, "tensor").reshape(users, items)
    return (beam_score, interest, logit)


def solution(mesh):
    placed = (
        P("user", None),
        P("user", BOTH),
        P("user", "leaf"),
        P(),
        P(BOTH, None),
        P(BOTH, None),
        P(),
        P(),
        P(),
        P(),
        P(None, "tensor"),
        P(None, None, "tensor"),
        P(None, "tensor"),
        P("tensor"),
    )
    return jax.shard_map(
        per_device,
        mesh=mesh,
        in_specs=placed,
        out_specs=(P("user", BOTH), P("user", None), P("user", "leaf")),
        check_vma=False,
    )
```

time: 350 us -> 146 us (0.42)
  waiting for transfers between devices: 233 us -> 2.5 us
  blocking collectives: 31.2 us -> 84.2 us
  local copies, waits for them, and re-layouts: 20.9 us -> 3.47 us
  starting transfers between devices: 20.6 us -> 6.43 us
  matrix products: 20.5 us -> 30.7 us
  other arithmetic: 8.75 us -> 3.65 us
    all_gather x2, waiting for transfers between devices: 225 us -> 1.8 us  [the longest x1 1.8 us: per_device(): proj_all = lax.all_gather(proj_in, 'tensor', axis=1, tiled=True)]
    all_gather x0 -> x4, blocking collectives: none -> 53.8 us  [the longest x1 21.6 us: per_device(): node_ids = lax.all_gather(beam_nodes.reshape(-1), BOTH, axis=0)]
    all_to_all x4 -> x1, starting transfers between devices: 20.4 us -> 6.35 us  [per_device(): lax.all_to_all(sent, BOTH, split_axis=0, concat_axis=0, tiled=True)]
    dot_general x5 -> x15, matrix products: 20.5 us -> 30.7 us  [the longest x1 6.74 us: per_device(): jnp.dot(item_rows, first_all[two:], preferred_element_type=F32)]
    gather x5 -> x0, local copies, waits for them, and re-layouts: 8.63 us -> none  [the longest x2 3.92 us: table_rows(): found = table[jnp.clip(wanted, 0, None)]]
    all_to_all x4 -> x1, waiting for transfers between devices: 7.35 us -> 0.01 us  [per_device(): lax.all_to_all(sent, BOTH, split_axis=0, concat_axis=0, tiled=True)]
    scatter x2 -> x0, local copies, waits for them, and re-layouts: 7.16 us -> none  [place_ids(): return jnp.full((total,), -1, jnp.int32).at[dest].set(values)]
  transfers between devices with their start and end apart: 6 -> 3, of which waited for: 4 -> 1; matrix products, arithmetic and copies ran while one was open for 6% -> 17% of each run, Pallas kernels for 0% -> 0%
where the time goes in v1:
time: 146 us; the launch traced here: 145 us
  blocking collectives  84.2 us (58%)
  matrix products  30.7 us (21%)
  between operations  14.2 us (10%)
  starting transfers between devices  6.43 us (4%)
  other arithmetic  3.65 us (2%)
  local copies, waits for them, and re-layouts  3.47 us (2%)
  waiting for transfers between devices  2.5 us (2%)
    all_gather x1, blocking collectives, per_device(): node_ids = lax.all_gather(beam_nodes.reshape(-1), BOTH, axis=0)  21.6 us
    psum x1, blocking collectives, per_device(): lax.psum(jnp.concatenate([numerator.reshape(-1), back.reshape(-1)]), BOTH)  21.1 us
    all_gather x1, blocking collectives, per_device(): item_rows = lax.all_gather(run_rows, 'tensor', axis=0, tiled=True)  14.2 us
    all_gather x1, blocking collectives, per_device(): bias_all = lax.all_gather(cross_b[0], 'tensor', axis=0, tiled=True)  12.6 us
    psum x1, blocking collectives, per_device(): logit = lax.psum(partial, 'tensor').reshape(users, items)  9.34 us
    dot_general x1, matrix products, per_device(): jnp.dot(item_rows, first_all[two:], preferred_element_type=F32)  6.74 us
    dot_general x1, matrix products, per_device(): jnp.dot(item_rows, proj_all[two:], preferred_element_type=F32)  6.37 us
    all_to_all x1, starting transfers between devices, per_device(): lax.all_to_all(sent, BOTH, split_axis=0, concat_axis=0, tiled=True)  6.35 us
  transfers between devices with their start and end apart: 3, of which 1 were waited for; matrix products, arithmetic and copies ran while one was open for 17% of the time, Pallas kernels for 0%

profile of v1, /device:TPU:0, one launch (start us, length us, event | category | flops | bytes accessed | tf_op | source)
XLA Modules:
  0.0 145.1 jit_solution(10727582794574176062)
XLA Ops:
  7.2 0.0 copy-start
  7.2 0.0 all-gather.6.cloned.1.call-start
  7.2 0.7 all-gather.6.cloned.1.call-update
  7.9 0.8 reshape.212
  8.7 5.3 %all-gather.2 = s32[2,1,1536]{2,1,0:T(1,128)S(1)} all-gather(s32[1,1,1536]{2,1,0:T(1,128)S(1)} %reshape.212), channel_id=1, replica_groups=mesh['leaf'=2,'user'=4,'tensor'=4] {'leaf'}, dimensions={0}, use_global_device_ids=true | all-gather | bytes 18432 | tf_op jit(solution)/shard_map/all_gather | solution.py:110
  14.1 0.8 select_reduce_fusion.1
  14.9 0.2 convolution_convert_fusion.3
  15.1 0.2 select_reduce_fusion
  15.4 0.1 sub.46
  15.4 0.0 copy-done
  15.4 1.3 fusion.18
  16.8 6.4 %all-to-all-start = ((bf16[8,48,128]{2,1,0:T(8,128)(2,1)}), bf16[8,48,128]{2,1,0:T(8,128)(2,1)S(1)}, u32[]{:S(2)}, u32[]{:S(2)}) async-start(bf16[8,48,128]{2,1,0:T(8,128)(2,1)} %bitcast.5), calls=%async_computation | async-start | bytes 196608 | tf_op jit(solution)/shard_map/all_to_all | solution.py:114
  23.1 0.0 all-gather.8.cloned.1.call-start
  23.2 0.8 reshape.210
  23.9 0.7 convert_element_type.72
  24.6 21.6 %all-gather.1 = s32[8,1,128]{2,1,0:T(1,128)S(1)} all-gather(s32[1,1,128]{2,1,0:T(1,128)S(1)} %reshape.210), channel_id=1, replica_groups=mesh['leaf'=2,'user'=4,'tensor'=4] {'leaf','tensor'}, dimensions={0}, use_global_device_ids=true | all-gather | bytes 4608 | tf_op jit(solution)/shard_map/all_gather | solution.py:80
  46.2 0.7 select_reduce_fusion.2
  47.0 0.1 convolution_convert_fusion.5
  47.1 0.3 select_reduce_fusion.4
  47.5 0.1 sub.42
  47.6 0.1 eq.153
  47.7 0.7 reshape.217
  48.3 1.3 fusion.19
  49.7 0.0 copy-start.5
  49.7 0.0 copy-start.6
  49.7 0.0 copy-start.7
  49.7 1.8 %all-gather.6.cloned.1.call-done = bf16[384,2048]{1,0:T(8,128)(2,1)} async-done(((bf16[384,512]{1,0:T(8,128)(2,1)}), bf16[384,2048]{1,0:T(8,128)(2,1)}) %all-gather.6.cloned.1.call-update) | async-done | bytes 1572880 | tf_op jit(solution)/shard_map/all_gather | solution.py:73
  51.5 3.8 %fusion.14 = bf16[384,512]{1,0:T(8,128)(2,1)} fusion(bf16[384,2048]{1,0:T(8,128)(2,1)} %all-gather.6.cloned.1.call-done, bf16[2,2048,512]{2,1,0:T(8,128)(2,1)} %param.25), kind=kOutput, calls=%fused_computation.19 | convolution fusion | flops 805502976 | bytes 4063232 | tf_op jit(solution)/shard_map/dot_general | solution.py:74
  55.3 0.0 copy-start.3
  55.3 0.0 copy-start.1
  55.3 0.0 copy-start.2
  55.3 0.0 all-gather.8.cloned.1.call-update
  55.4 0.0 copy-done.5
  55.4 1.0 convolution_convert_fusion.1
  56.3 0.0 copy-done.6
  56.3 0.0 copy-done.7
  56.3 1.2 add_divide_fusion
  57.5 0.1 broadcast_in_dim.117
  57.6 0.1 select_reduce_fusion.3
  57.7 1.1 convolution_bitcast_fusion
  58.8 21.1 %psum.14 = f32[2048]{0:T(1024)S(1)} all-reduce(f32[2048]{0:T(1024)S(1)} %pad_maximum_fusion), channel_id=1, replica_groups=mesh['leaf'=2,'user'=4,'tensor'=4] {'leaf','tensor'}, use_global_device_ids=true, to_apply=%region_4.5 | all-reduce | flops 2048 | bytes 16384 | tf_op jit(solution)/shard_map/psum | solution.py:101
  79.9 0.1 dynamic_slice.12
  80.0 0.7 reshape.204
  80.7 0.0 copy-done.3
  80.7 12.6 %all-gather = f32[1,2048]{1,0:T(1,128)S(1)} all-gather(f32[1,512]{1,0:T(1,128)S(1)} %get-tuple-element.10), channel_id=2, replica_groups=mesh['leaf'=2,'user'=4,'tensor'=4] {'tensor'}, dimensions={1}, use_global_device_ids=true | all-gather | bytes 10240 | tf_op jit(solution)/shard_map/all_gather | solution.py:76
  93.3 0.2 fusion.21
  93.5 0.6 fusion.63
  94.1 0.0 all-to-all-done
  94.1 0.3 convolution_convert_fusion
  94.4 14.2 %all_gather.20 = bf16[1536,128]{1,0:T(8,128)(2,1)S(1)} all-gather(bf16[384,128]{1,0:T(8,128)(2,1)S(1)} %convolution_convert_fusion), channel_id=1, replica_groups=mesh['leaf'=2,'user'=4,'tensor'=4] {'tensor'}, dimensions={0}, use_global_device_ids=true | all-gather | bytes 491520 | tf_op jit(solution)/shard_map/all_gather | solution.py:119
  108.6 0.0 copy-done.1
  108.6 0.0 copy-done.2
  108.6 0.2 fusion.23
  108.8 6.4 %bitcast_add_fusion.1 = f32[1536,2048]{1,0:T(8,128)} fusion(bf16[1536,128]{1,0:T(8,128)(2,1)S(1)} %all_gather.20, f32[8,2048]{1,0:T(8,128)S(1)} %fusion.23, bf16[384,2048]{1,0:T(8,128)(2,1)S(1)} %copy-done.1), kind=kOutput, calls=%fused_computation.3 | convolution fusion | flops 808452096 | bytes 13565952 | tf_op jit(solution)/shard_map/dot_general | solution.py:125
  115.2 0.0 all-gather.8.cloned.1.call-done
  115.2 1.5 %convolution_add_fusion.1 = f32[8,2048]{1,0:T(8,128)S(1)} fusion(bf16[384,2048]{1,0:T(8,128)(2,1)} %all-gather.8.cloned.1.call-done, f32[2048]{0:T(1024)S(1)} %bitcast.47, bf16[8,128]{1,0:T(8,128)(2,1)S(1)} %get-tuple-element.5, bf16[8,128]{1,0:T(8,128)(2,1)S(1)} %copy-done.2), kind=kOutput, calls=%fused_computation.11 | convolution fusion | flops 8413184 | bytes 1126400 | tf_op jit(solution)/shard_map/dot_general | solution.py:124
  116.7 0.0 copy-start.4
  116.7 6.7 %fusion = bf16[1536,2048]{1,0:T(8,128)(2,1)S(1)} fusion(f32[1536,2048]{1,0:T(8,128)} %bitcast_add_fusion.1, bf16[1536,128]{1,0:T(8,128)(2,1)S(1)} %all_gather.20, f32[8,2048]{1,0:T(8,128)S(1)} %convolution_add_fusion.1, bf16[384,2048]{1,0:T(8,128)(2,1)} %all-gather.8.cloned.1.call-done), kind=kOutput, calls=%fused_computation.1 | convolution fusion | flops 817889280 | bytes 19857408 | tf_op jit(solution)/shard_map/dot_general | solution.py:126
  123.4 0.0 copy-done.4
  123.4 5.4 %fusion.11 = f32[1536]{0:T(1024)S(1)} fusion(f32[512]{0:T(512)S(1)} %convert_element_type.72, bf16[1536,2048]{1,0:T(8,128)(2,1)S(1)} %fusion, s32[]{:T(128)S(6)} %select_n.127, f32[512]{0:T(512)S(1)} %bitcast.49, bf16[2,2048,512]{2,1,0:T(8,128)(2,1)S(1)} %copy-done.4, f32[1536,2048]{1,0:T(8,128)} %bitcast_add_fusion.1), kind=kOutput, calls=%fused_computation.18 | convolution fusion | flops 3226728960 | bytes 11544580 | tf_op jit(solution)/shard_map/dot_general | solution.py:130
  128.9 0.1 reshape.208
  129.0 9.3 %psum.15 = f32[8,192]{1,0:T(8,128)} all-reduce(f32[8,192]{1,0:T(8,128)S(1)} %reshape.208), channel_id=1, replica_groups=mesh['leaf'=2,'user'=4,'tensor'=4] {'tensor'}, use_global_device_ids=true, to_apply=%region_9.10 | all-reduce | flops 1536 | bytes 12288 | tf_op jit(solution)/shard_map/psum | solution.py:136
  (16 shorter events, 0.2 us)
Async XLA Ops:
  7.2 8.3 %copy-start = (bf16[2048,128]{1,0:T(8,128)(2,1)S(1)}, bf16[2048,128]{1,0:T(8,128)(2,1)}, u32[]{:S(2)}) copy-start(bf16[2048,128]{1,0:T(8,128)(2,1)} %param.19) | copy-start | bytes 1572868
  7.2 44.3 %all-gather.6.cloned.1.call-start = ((), (), s32[]{:S(2)}) async-start(), calls=%async_computation.1 | async-start | bytes 1966080 | tf_op jit(solution)/shard_map/all_gather | solution.py:73
  16.8 77.3 %all-to-all-start = ((bf16[8,48,128]{2,1,0:T(8,128)(2,1)}), bf16[8,48,128]{2,1,0:T(8,128)(2,1)S(1)}, u32[]{:S(2)}, u32[]{:S(2)}) async-start(bf16[8,48,128]{2,1,0:T(8,128)(2,1)} %bitcast.5), calls=%async_computation | async-start | bytes 196608 | tf_op jit(solution)/shard_map/all_to_all | solution.py:114
  23.1 92.1 %all-gather.8.cloned.1.call-start = ((), (), s32[]{:S(2)}) async-start(), calls=%async_computation.2 | async-start | bytes 1966080 | tf_op jit(solution)/shard_map/all_gather | solution.py:75
  49.7 5.7 %copy-start.5 = (bf16[2048,128]{1,0:T(8,128)(2,1)S(1)}, bf16[2048,128]{1,0:T(8,128)(2,1)}, u32[]{:S(2)}) copy-start(bf16[2048,128]{1,0:T(8,128)(2,1)} %param.18) | copy-start | bytes 1572868
  49.7 6.6 %copy-start.6 = (bf16[128,1024]{1,0:T(8,128)(2,1)S(1)}, bf16[128,1024]{1,0:T(8,128)(2,1)}, u32[]{:S(2)}) copy-start(bf16[128,1024]{1,0:T(8,128)(2,1)} %param.21) | copy-start | bytes 786436
  49.7 6.6 %copy-start.7 = (f32[1024]{0:T(1024)S(1)}, f32[1024]{0:T(1024)}, u32[]{:S(2)}) copy-start(f32[1024]{0:T(1024)} %param.22) | copy-start | bytes 12292
  55.3 25.3 %copy-start.3 = (f32[2,512]{1,0:T(2,128)S(1)}, f32[2,512]{1,0:T(2,128)}, u32[]{:S(2)}) copy-start(f32[2,512]{1,0:T(2,128)} %param.26) | copy-start | bytes 12292
  55.3 53.3 %copy-start.1 = (bf16[384,2048]{1,0:T(8,128)(2,1)S(1)}, bf16[384,2048]{1,0:T(8,128)(2,1)}, u32[]{:S(2)}) copy-start(bf16[384,2048]{1,0:T(8,128)(2,1)} %all-gather.6.cloned.1.call-done) | copy-start | bytes 4718596
  55.3 53.3 %copy-start.2 = (bf16[8,128]{1,0:T(8,128)(2,1)S(1)}, bf16[8,128]{1,0:T(8,128)(2,1)}, u32[]{:S(2)}) copy-start(bf16[8,128]{1,0:T(8,128)(2,1)} %param.14) | copy-start | bytes 6148
  116.7 6.7 %copy-start.4 = (bf16[2,2048,512]{2,1,0:T(8,128)(2,1)S(1)}, bf16[2,2048,512]{2,1,0:T(8,128)(2,1)}, u32[]{:S(2)}) copy-start(bf16[2,2048,512]{2,1,0:T(8,128)(2,1)} %param.25) | copy-start | bytes 12582916
Sparse Core Ops, SparseCore 0:
  9.6 41.9 all-gather.5
  55.5 37.4 all-gather.7

commit v2 on v1

v2 whole, which is shorter than its diff:
```python
import functools
import math

import jax
import jax.numpy as jnp
from jax import lax
from jax.experimental import pallas as pl
from jax.experimental.pallas import tpu as pltpu
from jax.sharding import PartitionSpec as P

SUB_NODES = 512
SUB_ITEMS = 512
BOTH = ("leaf", "tensor")
F32 = jnp.float32
BF16 = jnp.bfloat16


def small_lookup(table, index):
    hits = index[..., None] == jnp.arange(table.shape[0], dtype=jnp.int32)
    return jnp.sum(jnp.where(hits, table, 0), axis=-1)


def locate(ids, span, subtree_slot, rows):
    slot = small_lookup(subtree_slot, ids // span)
    per = rows // span
    return slot // per, slot % per * span + ids % span


def rank_in_row(marks):
    n = marks.shape[-1]
    at = jnp.arange(n, dtype=jnp.int32)
    before = (at[:, None] < at[None, :]).astype(BF16)
    return jnp.dot(marks.astype(BF16), before, preferred_element_type=F32).astype(jnp.int32)


def pick_rows(table, wanted):
    hot = (wanted[:, None] == jnp.arange(table.shape[0], dtype=jnp.int32)[None, :]).astype(BF16)
    return jnp.dot(hot, table, preferred_element_type=F32).astype(BF16)


def exchange_kernel(modes, leafs, tensors, wide, *refs):
    n = len(modes)
    srcs, outs, send_sems, recv_sems = refs[:n], refs[n : 2 * n], refs[2 * n], refs[2 * n + 1]
    leaf, tensor = lax.axis_index("leaf"), lax.axis_index("tensor")
    size = leafs * tensors if wide else tensors
    me = leaf * tensors + tensor if wide else tensor

    def target(k):
        peer = (me + k) % size
        if wide:
            return peer, peer // tensors, peer % tensors
        return peer, leaf, peer

    def part(mode, src, peer, peer_leaf):
        if mode == "peer":
            return src.at[peer]
        if mode == "leaf":
            return src.at[peer_leaf]
        return src

    def copies(k):
        peer, peer_leaf, peer_tensor = target(k)
        return [
            pltpu.make_async_remote_copy(
                src_ref=part(mode, src, peer, peer_leaf),
                dst_ref=out.at[me],
                send_sem=send_sems.at[i, k - 1],
                recv_sem=recv_sems.at[i, k - 1],
                device_id={"leaf": peer_leaf, "tensor": peer_tensor},
                device_id_type=pl.DeviceIdType.MESH,
            )
            for i, (mode, src, out) in enumerate(zip(modes, srcs, outs))
        ]

    barrier = pltpu.get_barrier_semaphore()

    @pl.loop(1, size)
    def _(k):
        _, peer_leaf, peer_tensor = target(k)
        pl.semaphore_signal(
            barrier,
            inc=1,
            device_id={"leaf": peer_leaf, "tensor": peer_tensor},
            device_id_type=pl.DeviceIdType.MESH,
        )

    pl.semaphore_wait(barrier, size - 1)

    @pl.loop(1, size)
    def _(k):
        for copy in copies(k):
            copy.start()

    for mode, src, out in zip(modes, srcs, outs):
        out[me] = part(mode, src, me, leaf)[...]

    @pl.loop(1, size)
    def _(k):
        for copy in copies(k):
            copy.wait()


def exchange(collective_id, wide, *entries):
    leafs, tensors = lax.axis_size("leaf"), lax.axis_size("tensor")
    size = leafs * tensors if wide else tensors
    modes = tuple(mode for mode, _ in entries)
    arrays = [array for _, array in entries]
    outs = [
        jax.ShapeDtypeStruct((size,) + (a.shape if mode == "all" else a.shape[1:]), a.dtype)
        for mode, a in entries
    ]
    return pl.pallas_call(
        functools.partial(exchange_kernel, modes, leafs, tensors, wide),
        out_shape=outs,
        in_specs=[pl.BlockSpec(memory_space=pltpu.VMEM)] * len(arrays),
        out_specs=[pl.BlockSpec(memory_space=pltpu.VMEM)] * len(arrays),
        scratch_shapes=[
            pltpu.SemaphoreType.DMA((len(arrays), size - 1)),
            pltpu.SemaphoreType.DMA((len(arrays), size - 1)),
        ],
        compiler_params=pltpu.CompilerParams(
            collective_id=collective_id, has_side_effects=True, vmem_limit_bytes=32 << 20
        ),
    )(*arrays)


def rank_kernel_body(
    tensors, rows_ref, proj_ref, first_ref, own_proj, own_first, base0, base1, own0, own1,
    cross, bias, weight, out_ref,
):
    rows = rows_ref[0]
    cols = own_proj.shape[1]
    dot = functools.partial(jnp.dot, preferred_element_type=F32)
    second = jnp.zeros((rows.shape[0], cols), F32)
    for t in range(tensors):
        x0 = dot(rows, proj_ref[t]) + base0[0, t : t + 1]
        mixed = dot(rows, first_ref[t]) + base1[0, t : t + 1]
        x1 = (x0 * mixed + x0).astype(BF16)
        second += dot(x1, cross[t * cols : (t + 1) * cols, :])
    x0 = dot(rows, own_proj[...]) + own0[0]
    x1 = x0 * (dot(rows, own_first[...]) + own1[0]) + x0
    x2 = x0 * (second + bias[...]) + x1
    out_ref[0] = lax.dot_general(
        weight[...], x2, (((1,), (1,)), ((), ())),
        precision=lax.Precision.HIGHEST, preferred_element_type=F32,
    )


def rank_rows(rows, proj_all, first_all, proj, first, base0, base1, own0, own1, cross, bias, weight):
    users, items, width = rows.shape
    tensors, _, cols = proj_all.shape
    full3 = pl.BlockSpec((tensors, width, cols), lambda u: (0, 0, 0))
    own = pl.BlockSpec((width, cols), lambda u: (0, 0))
    line = pl.BlockSpec((1, cols), lambda u: (0, 0))
    return pl.pallas_call(
        functools.partial(rank_kernel_body, tensors),
        grid=(users,),
        out_shape=jax.ShapeDtypeStruct((users, 1, items), F32),
        in_specs=[
            pl.BlockSpec((1, items, width), lambda u: (u, 0, 0)),
            full3, full3, own, own,
            pl.BlockSpec((1, tensors, cols), lambda u: (u, 0, 0)),
            pl.BlockSpec((1, tensors, cols), lambda u: (u, 0, 0)),
            pl.BlockSpec((1, 1, cols), lambda u: (u, 0, 0)),
            pl.BlockSpec((1, 1, cols), lambda u: (u, 0, 0)),
            pl.BlockSpec(cross.shape, lambda u: (0, 0)),
            line, line,
        ],
        out_specs=pl.BlockSpec((1, 1, items), lambda u: (u, 0, 0)),
        compiler_params=pltpu.CompilerParams(vmem_limit_bytes=40 << 20),
    )(rows, proj_all, first_all, proj, first, base0, base1, own0, own1, cross, bias, weight)


def request_lists(owner, coded, owners, cap):
    marks = owner[None, :] == jnp.arange(owners, dtype=jnp.int32)[:, None]
    rank = rank_in_row(marks)
    chosen = marks[:, None, :] & (
        rank[:, None, :] == jnp.arange(cap, dtype=jnp.int32)[None, :, None]
    )
    return chosen, jnp.sum(jnp.where(chosen, coded + 1, 0), axis=2) - 1


def per_device(
    user_feat,
    beam_nodes,
    item_ids,
    subtree_slot,
    node_table,
    item_table,
    mlp_user,
    mlp_node,
    mlp_bias,
    mlp_out,
    proj_in,
    cross_w,
    cross_b,
    out_w,
):
    leafs = lax.axis_size("leaf")
    tensors = lax.axis_size("tensor")
    owners = leafs * tensors
    tensor_at = lax.axis_index("tensor")
    users, beam = beam_nodes.shape
    items = item_ids.shape[1]
    width = user_feat.shape[1]
    two = 2 * width
    cols = proj_in.shape[1]

    proj_here = proj_in[two:]
    proj_all = lax.all_gather(proj_here, "tensor", axis=0)
    flat_proj = jnp.moveaxis(proj_all, 0, 1).reshape(width, tensors * cols)
    first_here = jnp.dot(flat_proj, cross_w[0], preferred_element_type=F32).astype(BF16)
    first_all = lax.all_gather(first_here, "tensor", axis=0)

    requests = users * beam
    cap_b = max(2, -(-requests // owners))
    n_owner, n_local = locate(beam_nodes.reshape(-1), SUB_NODES, subtree_slot, node_table.shape[0])
    asker = jnp.arange(requests, dtype=jnp.int32) // beam
    n_chosen, n_list = request_lists(n_owner, n_local * users + asker, owners, cap_b)
    rows = users * items
    fetch = rows // tensors
    cap_i = max(2, -(-fetch // owners))
    i_owner, i_local = locate(item_ids.reshape(-1), SUB_ITEMS, subtree_slot, item_table.shape[0])
    i_owner, i_local = i_owner.reshape(tensors, fetch), i_local.reshape(tensors, fetch)
    run_owner = lax.dynamic_slice(i_owner, (tensor_at, 0), (1, fetch))[0]
    run_local = lax.dynamic_slice(i_local, (tensor_at, 0), (1, fetch))[0]
    _, i_list = request_lists(run_owner, run_local, owners, cap_i)
    lists = jnp.concatenate([n_list, i_list], axis=1)
    lanes = -(-lists.shape[1] // 128) * 128
    lists = jnp.pad(lists, ((0, 0), (0, lanes - lists.shape[1])))[:, None, :]
    (asked,) = exchange(0, True, ("peer", lists))
    n_asked = asked[:, 0, :cap_b].reshape(-1)
    i_asked = asked[:, 0, cap_b : cap_b + cap_i].reshape(-1)

    sent = pick_rows(item_table, i_asked).reshape(leafs, tensors * cap_i, width)
    held = n_asked >= 0
    node_rows = pick_rows(node_table, jnp.where(held, n_asked // users, -1))
    user_hot = (n_asked % users)[:, None] == jnp.arange(users, dtype=jnp.int32)[None, :]
    user_rows = jnp.dot(user_hot.astype(BF16), user_feat, preferred_element_type=F32).astype(BF16)
    pre = (
        jnp.dot(user_rows, mlp_user, preferred_element_type=F32)
        + jnp.dot(node_rows, mlp_node, preferred_element_type=F32)
        + mlp_bias
    )
    hidden = jax.nn.silu(pre).astype(BF16)
    scores = jnp.dot(hidden, mlp_out, preferred_element_type=F32)
    gate = jnp.where(user_hot & held[:, None], jax.nn.sigmoid(scores)[:, None], 0.0)
    numerator = lax.dot_general(
        gate, node_rows.astype(F32), (((0,), (0,)), ((), ())), precision=lax.Precision.HIGHEST
    )
    back_lanes = -(-cap_b // 128) * 128
    back = jnp.pad(scores.reshape(owners, cap_b), ((0, 0), (0, back_lanes - cap_b)))[:, None, :]
    sums, scored, arrived = exchange(
        1, True, ("all", numerator), ("peer", back), ("leaf", sent)
    )
    interest = jnp.sum(sums, axis=0) / math.sqrt(owners * beam)
    own_scores = scored[:, 0, :cap_b]
    beam_score = jnp.sum(
        jnp.where(n_chosen, own_scores[:, :, None], 0.0), axis=(0, 1)
    ).reshape(users, beam)

    shared = jnp.concatenate([user_feat, interest.astype(BF16)], axis=1)
    own0 = jnp.dot(shared, proj_in[:two], preferred_element_type=F32)
    (all0,) = exchange(2, False, ("all", own0))
    base0 = jnp.moveaxis(all0, 0, 1)
    flat0 = base0.reshape(users, tensors * cols).astype(BF16)
    own1 = jnp.dot(flat0, cross_w[0], preferred_element_type=F32) + cross_b[0]
    (all1,) = exchange(3, False, ("all", own1))
    base1 = jnp.moveaxis(all1, 0, 1)

    run_marks = i_owner[:, None, :] == jnp.arange(owners, dtype=jnp.int32)[None, :, None]
    run_rank = jnp.sum(jnp.where(run_marks, rank_in_row(run_marks), 0), axis=1)
    place = run_rank + i_owner * cap_i
    by_run = jnp.moveaxis(arrived.reshape(owners, tensors, cap_i, width), 1, 0)
    hot = (place[:, :, None] == jnp.arange(owners * cap_i, dtype=jnp.int32)).astype(BF16)
    item_rows = jnp.einsum(
        "tfs,tsd->tfd", hot, by_run.reshape(tensors, owners * cap_i, width),
        preferred_element_type=F32,
    ).astype(BF16).reshape(users, items, width)

    partial = rank_rows(
        item_rows, proj_all, first_all, proj_here, first_here, base0, base1,
        own0[:, None, :], own1[:, None, :], cross_w[1], cross_b[1][None, :],
        out_w.astype(F32)[None, :],
    )
    (parts,) = exchange(4, False, ("all", partial.reshape(users, items)))
    logit = jnp.sum(parts, axis=0)
    return (beam_score, interest, logit)


def solution(mesh):
    placed = (
        P("user", None),
        P("user", BOTH),
        P("user", "leaf"),
        P(),
        P(BOTH, None),
        P(BOTH, None),
        P(),
        P(),
        P(),
        P(),
        P(None, "tensor"),
        P(None, None, "tensor"),
        P(None, "tensor"),
        P("tensor"),
    )
    return jax.shard_map(
        per_device,
        mesh=mesh,
        in_specs=placed,
        out_specs=(P("user", BOTH), P("user", None), P("user", "leaf")),
        check_vma=False,
    )
```

time: 146 us -> 106 us (0.73)
  Pallas kernels: 0 us -> 55.8 us
  blocking collectives: 84.2 us -> 31 us
  matrix products: 30.7 us -> 8.39 us
  between operations: 14.2 us -> 0.97 us
  starting transfers between devices: 6.43 us -> 0 us
  waiting for transfers between devices: 2.5 us -> 0 us
  local copies, waits for them, and re-layouts: 3.47 us -> 5.57 us
    pallas_call x0 -> x6, Pallas kernels: none -> 55.8 us  [the longest x5 38.3 us: exchange(): pl.pallas_call(functools.partial(exchange_kernel, modes, leafs, tensors,...]
    psum x2 -> x0, blocking collectives: 30.4 us -> none  [the longest x1 21.1 us: per_device(): lax.psum(jnp.concatenate([numerator.reshape(-1), back.reshape(-1)]), BOTH)]
    all_gather x4 -> x2, blocking collectives: 53.8 us -> 31 us  [the longest x1 15.7 us: per_device(): first_all = lax.all_gather(first_here, 'tensor', axis=0)]
    dot_general x6 -> x4, matrix products: 24 us -> 4.73 us  [the longest x1 2.06 us: per_device(): jnp.dot(flat_proj, cross_w[0], preferred_element_type=F32).astype(BF16)]
    all_to_all x1 -> x0, starting transfers between devices: 6.35 us -> none  [per_device(): lax.all_to_all(sent, BOTH, split_axis=0, concat_axis=0, tiled=True)]
    reshape x3 -> x5, local copies, waits for them, and re-layouts: 0.77 us -> 3.14 us  [the longest x2 1.54 us: per_device(): item_ids.reshape(-1)]
    all_gather x2 -> x0, waiting for transfers between devices: 1.8 us -> none  [the longest x1 1.8 us: per_device(): proj_all = lax.all_gather(proj_in, 'tensor', axis=1, tiled=True)]
    unnamed x19 -> x17, local copies, waits for them, and re-layouts: 2.28 us -> 0.75 us
  transfers between devices with their start and end apart: 3 -> 0, of which waited for: 1 -> 0; matrix products, arithmetic and copies ran while one was open for 17% -> 0% of each run, Pallas kernels for 0% -> 0%
where the time goes in v2:
time: 106 us
  Pallas kernels  55.8 us (53%)
  blocking collectives  31 us (29%)
  matrix products  8.39 us (8%)
  local copies, waits for them, and re-layouts  5.57 us (5%)
  other arithmetic  4.22 us (4%)
    pallas_call x5, Pallas kernels, exchange(): pl.pallas_call(functools.partial(exchange_kernel, modes, leafs, tensors,...  38.3 us
    pallas_call x1, Pallas kernels, rank_rows(): pl.pallas_call(functools.partial(rank_kernel_body, tensors), grid=(users,...  17.4 us
    all_gather x1, blocking collectives, per_device(): first_all = lax.all_gather(first_here, 'tensor', axis=0)  15.7 us
    all_gather x1, blocking collectives, per_device(): proj_all = lax.all_gather(proj_here, 'tensor', axis=0)  15.3 us

profile of v2, /device:TPU:0, one launch (start us, length us, event | category | flops | bytes accessed | tf_op | source)
XLA Modules:
  0.0 105.9 jit_solution(2473301820672392846)
XLA Ops:
  0.6 0.0 copy-start
  0.6 0.0 copy-start.2
  0.7 0.8 reshape.278
  1.5 0.7 select_reduce_fusion.4
  2.3 0.7 broadcast_in_dim.131
  3.0 0.1 convolution_convert_fusion.4
  3.1 0.2 select_reduce_fusion.3
  3.3 0.7 reshape.292
  4.0 0.8 fusion.60
  4.8 0.8 reshape.280
  5.6 0.8 reshape.279
  6.4 0.8 select_reduce_fusion.1
  7.2 0.2 fusion.18
  7.4 0.1 convolution_convert_fusion.3
  7.5 0.3 select_reduce_fusion
  7.8 0.1 pad_add_fusion
  7.9 8.4 %shard_map.157 = s32[8,1,128]{2,1,0:T(1,128)S(1)} custom-call(s32[8,1,128]{2,1,0:T(1,128)S(1)} %bitcast.69), custom_call_target="tpu_custom_call" | custom-call | tf_op jit(solution)/shard_map/pallas_call | solution.py:112
  16.3 0.1 slice_reduce_fusion
  16.4 0.1 eq.187
  16.5 0.1 reshape_squeeze.3
  16.6 1.4 %convolution_convert_fusion.1 = bf16[128,128]{1,0:T(8,128)(2,1)S(1)} fusion(bf16[2048,128]{1,0:T(8,128)(2,1)} %param.18, s32[128]{0:T(128)S(1)} %get-tuple-element.17), kind=kOutput, calls=%fused_computation.20 | convolution fusion | flops 67387392 | bytes 557568 | tf_op jit(solution)/shard_map/dot_general | solution.py:38
  18.0 0.0 copy-done
  18.1 0.7 fusion.15
  18.7 0.0 copy-start.3
  18.8 0.0 copy-start.4
  18.8 0.0 copy-start.5
  18.8 0.0 copy-start.6
  18.8 0.0 copy-done.2
  18.8 15.3 %all-gather = bf16[512,512]{1,0:T(8,128)(2,1)S(1)} all-gather(bf16[128,512]{1,0:T(8,128)(2,1)S(1)} %slice.31.own_proj), channel_id=2, replica_groups=mesh['leaf'=2,'user'=4,'tensor'=4] {'tensor'}, dimensions={0}, use_global_device_ids=true | all-gather | bytes 655360 | tf_op jit(solution)/shard_map/all_gather | solution.py:210
  34.1 0.3 copy.25
  34.4 2.1 %fusion.12.own_first = bf16[128,512]{1,0:T(8,128)(2,1)S(1)} fusion(bf16[128,2048]{0,1:T(8,128)(2,1)S(1)} %bitcast.73, bf16[2,2048,512]{2,1,0:T(8,128)(2,1)} %param.25), kind=kOutput, calls=%fused_computation.16 | convolution fusion | flops 268500992 | bytes 2752512 | tf_op jit(solution)/shard_map/dot_general | solution.py:212
  36.4 15.7 %all-gather.1 = bf16[512,512]{1,0:T(8,128)(2,1)S(1)} all-gather(bf16[128,512]{1,0:T(8,128)(2,1)S(1)} %fusion.12.own_first), channel_id=3, replica_groups=mesh['leaf'=2,'user'=4,'tensor'=4] {'tensor'}, dimensions={0}, use_global_device_ids=true | all-gather | bytes 655360 | tf_op jit(solution)/shard_map/all_gather | solution.py:213
  52.1 0.0 copy-done.3
  52.1 0.0 copy-done.4
  52.1 0.4 fusion.17
  52.5 0.0 copy-done.5
  52.5 0.0 copy-done.6
  52.5 0.4 add_divide_fusion
  52.9 0.4 fusion.30.refs_0_
  53.3 0.1 reshape.281
  53.4 12.5 %shard_map.158 = (f32[8,8,128]{2,1,0:T(8,128)S(1)}, f32[8,1,128]{2,1,0:T(1,128)S(1)}, bf16[8,192,128]{2,1,0:T(8,128)(2,1)S(1)}) custom-call(f32[8,128]{1,0:T(8,128)S(1)} %fusion.30.refs_0_, f32[8,1,128]{2,1,0:T(1,128)S(1)} %bitcast.70, bf16[2,192,128]{2,1,0:T(8,128)(2,1)S(1)} %bitcast.67), custom_call_target="tpu_custom_call" | custom-call | tf_op jit(solution)/shard_map/pallas_call | solution.py:112
  65.9 0.1 select_reduce_fusion.2
  66.0 0.7 reshape.283
  66.7 0.0 copy-start.1
  66.7 0.6 fusion.59
  67.3 0.1 fusion.26.refs_0_
  67.4 5.8 %shard_map.159 = f32[4,8,512]{2,1,0:T(8,128)S(1)} custom-call(f32[8,512]{1,0:T(8,128)S(1)} %fusion.26.refs_0_), custom_call_target="tpu_custom_call" | custom-call | tf_op jit(solution)/shard_map/pallas_call | solution.py:112
  73.3 2.0 %fusion.19.refs_0_ = f32[8,512]{1,0:T(8,128)S(1)} fusion(bf16[8,2048]{1,0:T(8,128)(2,1)S(1)} %bitcast.75, bf16[2,2048,512]{2,1,0:T(8,128)(2,1)} %param.25, f32[512]{0:T(512)S(1)} %bitcast.77), kind=kOutput, calls=%fused_computation.24 | convolution fusion | flops 16781312 | bytes 2148352 | tf_op jit(solution)/shard_map/dot_general | solution.py:267
  75.3 6.0 %shard_map.160 = f32[4,8,512]{2,1,0:T(8,128)S(1)} custom-call(f32[8,512]{1,0:T(8,128)S(1)} %fusion.19.refs_0_), custom_call_target="tpu_custom_call" | custom-call | tf_op jit(solution)/shard_map/pallas_call | solution.py:112
  81.4 0.6 fusion.9
  82.0 0.0 copy-done.1
  82.0 0.1 slice_bitcast_fusion.cross
  82.1 17.4 %shard_map.161 = f32[8,1,192]{2,1,0:T(1,128)S(1)} custom-call(bf16[8,192,128]{2,1,0:T(8,128)(2,1)S(1)} %bitcast.63, bf16[4,128,512]{2,1,0:T(8,128)(2,1)S(1)} %bitcast.61, bf16[4,128,512]{2,1,0:T(8,128)(2,1)S(1)} %bitcast.62, bf16[128,512]{1,0:T(8,128)(2,1)S(1)} %slice.31.own_proj, bf16[128,512]{1,0:T(8,128)(2,1)S(1)} %fusion.12.own_first, ...), custom_call_target="tpu_custom_call" | custom-call | tf_op jit(solution)/shard_map/pallas_call | solution.py:155
  99.6 5.7 %shard_map.162 = f32[4,8,192]{2,1,0:T(8,128)S(1)} custom-call(f32[8,192]{1,0:T(8,128)S(1)} %bitcast.68), custom_call_target="tpu_custom_call" | custom-call | tf_op jit(solution)/shard_map/pallas_call | solution.py:112
  105.3 0.6 reduce_sum.82
  (28 shorter events, 0.4 us)
Async XLA Ops:
  0.6 17.4 %copy-start = (bf16[2048,128]{1,0:T(8,128)(2,1)S(1)}, bf16[2048,128]{1,0:T(8,128)(2,1)}, u32[]{:S(2)}) copy-start(bf16[2048,128]{1,0:T(8,128)(2,1)} %param.19) | copy-start | bytes 1572868
  0.6 18.2 %copy-start.2 = (bf16[384,512]{1,0:T(8,128)(2,1)S(1)}, bf16[384,512]{1,0:T(8,128)(2,1)}, u32[]{:S(2)}) copy-start(bf16[384,512]{1,0:T(8,128)(2,1)} %param.24) | copy-start | bytes 1179652
  18.7 33.4 %copy-start.3 = (bf16[128,1024]{1,0:T(8,128)(2,1)S(1)}, bf16[128,1024]{1,0:T(8,128)(2,1)}, u32[]{:S(2)}) copy-start(bf16[128,1024]{1,0:T(8,128)(2,1)} %param.20) | copy-start | bytes 786436
  18.8 33.4 %copy-start.4 = (bf16[8,128]{1,0:T(8,128)(2,1)S(1)}, bf16[8,128]{1,0:T(8,128)(2,1)}, u32[]{:S(2)}) copy-start(bf16[8,128]{1,0:T(8,128)(2,1)} %param.14) | copy-start | bytes 6148
  18.8 33.8 %copy-start.5 = (bf16[128,1024]{1,0:T(8,128)(2,1)S(1)}, bf16[128,1024]{1,0:T(8,128)(2,1)}, u32[]{:S(2)}) copy-start(bf16[128,1024]{1,0:T(8,128)(2,1)} %param.21) | copy-start | bytes 786436
  18.8 33.8 %copy-start.6 = (f32[1024]{0:T(1024)S(1)}, f32[1024]{0:T(1024)}, u32[]{:S(2)}) copy-start(f32[1024]{0:T(1024)} %param.22) | copy-start | bytes 12292
  66.7 15.3 %copy-start.1 = (bf16[2,2048,512]{2,1,0:T(8,128)(2,1)S(1)}, bf16[2,2048,512]{2,1,0:T(8,128)(2,1)}, u32[]{:S(2)}) copy-start(bf16[2,2048,512]{2,1,0:T(8,128)(2,1)} %param.25) | copy-start | bytes 12582916

commit v3 on v2

--- a/solution.py
+++ b/solution.py
@@ -38,18 +38,28 @@
     return jnp.dot(hot, table, preferred_element_type=F32).astype(BF16)
 
 
-def exchange_kernel(modes, leafs, tensors, wide, *refs):
+def exchange_kernel(modes, sizes, *refs):
     n = len(modes)
-    srcs, outs, send_sems, recv_sems = refs[:n], refs[n : 2 * n], refs[2 * n], refs[2 * n + 1]
-    leaf, tensor = lax.axis_index("leaf"), lax.axis_index("tensor")
-    size = leafs * tensors if wide else tensors
-    me = leaf * tensors + tensor if wide else tensor
-
-    def target(k):
-        peer = (me + k) % size
-        if wide:
-            return peer, peer // tensors, peer % tensors
-        return peer, leaf, peer
+    srcs, outs, send_sems, recv_sems = refs[:n], refs[n : 2 * n], refs[2 * n : 3 * n], refs[3 * n :]
+    leaf, tensor, user = (lax.axis_index(axis) for axis in ("leaf", "tensor", "user"))
+    leafs, tensors, users = sizes
+
+    def group_of(mode):
+        if mode in ("tensor", "user"):
+            return mode
+        return "wide"
+
+    def extent(group):
+        return {"wide": leafs * tensors, "tensor": tensors, "user": users}[group]
+
+    def index(group):
+        return {"wide": leaf * tensors + tensor, "tensor": tensor, "user": user}[group]
+
+    def target(group, k):
+        peer = (index(group) + k) % extent(group)
+        if group == "wide":
+            return peer, {"leaf": peer // tensors, "tensor": peer % tensors}
+        return peer, {group: peer}
 
     def part(mode, src, peer, peer_leaf):
         if mode == "peer":
@@ -58,66 +68,73 @@
             return src.at[peer_leaf]
         return src
 
-    def copies(k):
-        peer, peer_leaf, peer_tensor = target(k)
-        return [
-            pltpu.make_async_remote_copy(
-                src_ref=part(mode, src, peer, peer_leaf),
-                dst_ref=out.at[me],
-                send_sem=send_sems.at[i, k - 1],
-                recv_sem=recv_sems.at[i, k - 1],
-                device_id={"leaf": peer_leaf, "tensor": peer_tensor},
+    def copy(i, k):
+        group = group_of(modes[i])
+        peer, place = target(group, k)
+        return pltpu.make_async_remote_copy(
+            src_ref=part(modes[i], srcs[i], peer, place.get("leaf")),
+            dst_ref=outs[i].at[index(group)],
+            send_sem=send_sems[i].at[k - 1],
+            recv_sem=recv_sems[i].at[k - 1],
+            device_id=place,
+            device_id_type=pl.DeviceIdType.MESH,
+        )
+
+    members = {}
+    for i, mode in enumerate(modes):
+        members.setdefault(group_of(mode), []).append(i)
+    greeted = [g for g in members if not (g == "tensor" and "wide" in members)]
+
+    barrier = pltpu.get_barrier_semaphore()
+    for group in greeted:
+
+        @pl.loop(1, extent(group))
+        def _(k):
+            pl.semaphore_signal(
+                barrier,
+                inc=1,
+                device_id=target(group, k)[1],
                 device_id_type=pl.DeviceIdType.MESH,
             )
-            for i, (mode, src, out) in enumerate(zip(modes, srcs, outs))
-        ]
-
-    barrier = pltpu.get_barrier_semaphore()
-
-    @pl.loop(1, size)
-    def _(k):
-        _, peer_leaf, peer_tensor = target(k)
-        pl.semaphore_signal(
-            barrier,
-            inc=1,
-            device_id={"leaf": peer_leaf, "tensor": peer_tensor},
-            device_id_type=pl.DeviceIdType.MESH,
-        )
-
-    pl.semaphore_wait(barrier, size - 1)
-
-    @pl.loop(1, size)
-    def _(k):
-        for copy in copies(k):
-            copy.start()
+
+    pl.semaphore_wait(barrier, sum(extent(group) - 1 for group in greeted))
+
+    for group, held in members.items():
+
+        @pl.loop(1, extent(group))
+        def _(k):
+            for i in held:
+                copy(i, k).start()
 
     for mode, src, out in zip(modes, srcs, outs):
-        out[me] = part(mode, src, me, leaf)[...]
-
-    @pl.loop(1, size)
-    def _(k):
-        for copy in copies(k):
-            copy.wait()
-
-
-def exchange(collective_id, wide, *entries):
-    leafs, tensors = lax.axis_size("leaf"), lax.axis_size("tensor")
-    size = leafs * tensors if wide else tensors
+        at = index(group_of(mode))
+        out[at] = part(mode, src, at, leaf)[...]
+
+    for group, held in members.items():
+
+        @pl.loop(1, extent(group))
+        def _(k):
+            for i in held:
+                copy(i, k).wait()
+
+
+def exchange(collective_id, *entries):
+    sizes = tuple(lax.axis_size(axis) for axis in ("leaf", "tensor", "user"))
     modes = tuple(mode for mode, _ in entries)
     arrays = [array for _, array in entries]
+    extents = [{"tensor": sizes[1], "user": sizes[2]}.get(m, sizes[0] * sizes[1]) for m in modes]
     outs = [
-        jax.ShapeDtypeStruct((size,) + (a.shape if mode == "all" else a.shape[1:]), a.dtype)
-        for mode, a in entries
+        jax.ShapeDtypeStruct(
+            (size,) + (a.shape[1:] if mode in ("peer", "leaf") else a.shape), a.dtype
+        )
+        for mode, a, size in zip(modes, arrays, extents)
     ]
     return pl.pallas_call(
-        functools.partial(exchange_kernel, modes, leafs, tensors, wide),
+        functools.partial(exchange_kernel, modes, sizes),
         out_shape=outs,
         in_specs=[pl.BlockSpec(memory_space=pltpu.VMEM)] * len(arrays),
         out_specs=[pl.BlockSpec(memory_space=pltpu.VMEM)] * len(arrays),
-        scratch_shapes=[
-            pltpu.SemaphoreType.DMA((len(arrays), size - 1)),
-            pltpu.SemaphoreType.DMA((len(arrays), size - 1)),
-        ],
+        scratch_shapes=[pltpu.SemaphoreType.DMA((size - 1,)) for size in extents] * 2,
         compiler_params=pltpu.CompilerParams(
             collective_id=collective_id, has_side_effects=True, vmem_limit_bytes=32 << 20
         ),
@@ -128,46 +145,53 @@
     tensors, rows_ref, proj_ref, first_ref, own_proj, own_first, base0, base1, own0, own1,
     cross, bias, weight, out_ref,
 ):
-    rows = rows_ref[0]
+    users, items, width = rows_ref.shape
+    rows = rows_ref[...].reshape(users * items, width)
     cols = own_proj.shape[1]
-    dot = functools.partial(jnp.dot, preferred_element_type=F32)
-    second = jnp.zeros((rows.shape[0], cols), F32)
+
+    def dot(left, right):
+        return jnp.dot(left, right, preferred_element_type=F32)
+
+    def layer(proj, first, add0, add1):
+        x0 = dot(rows, proj).reshape(users, items, cols) + add0
+        return x0, x0 * (dot(rows, first).reshape(users, items, cols) + add1) + x0
+
+    second = jnp.zeros((users * items, cols), F32)
     for t in range(tensors):
-        x0 = dot(rows, proj_ref[t]) + base0[0, t : t + 1]
-        mixed = dot(rows, first_ref[t]) + base1[0, t : t + 1]
-        x1 = (x0 * mixed + x0).astype(BF16)
+        proj = proj_ref[:, t].reshape(width, cols)
+        first = first_ref[:, t].reshape(width, cols)
+        _, x1 = layer(proj, first, base0[:, t : t + 1], base1[:, t : t + 1])
+        x1 = x1.astype(BF16).reshape(users * items, cols)
         second += dot(x1, cross[t * cols : (t + 1) * cols, :])
-    x0 = dot(rows, own_proj[...]) + own0[0]
-    x1 = x0 * (dot(rows, own_first[...]) + own1[0]) + x0
-    x2 = x0 * (second + bias[...]) + x1
-    out_ref[0] = lax.dot_general(
-        weight[...], x2, (((1,), (1,)), ((), ())),
-        precision=lax.Precision.HIGHEST, preferred_element_type=F32,
-    )
+    x0, x1 = layer(own_proj[...], own_first[...], own0[...], own1[...])
+    x2 = x0 * (second.reshape(users, items, cols) + bias[...]) + x1
+    out_ref[0] = jnp.sum(x2 * weight[...], axis=2)
 
 
 def rank_rows(rows, proj_all, first_all, proj, first, base0, base1, own0, own1, cross, bias, weight):
     users, items, width = rows.shape
-    tensors, _, cols = proj_all.shape
-    full3 = pl.BlockSpec((tensors, width, cols), lambda u: (0, 0, 0))
+    tensors = proj_all.shape[1]
+    cols = proj.shape[1]
+    step = math.gcd(users, 4)
+    full = pl.BlockSpec(proj_all.shape, lambda u: (0, 0, 0, 0))
     own = pl.BlockSpec((width, cols), lambda u: (0, 0))
     line = pl.BlockSpec((1, cols), lambda u: (0, 0))
     return pl.pallas_call(
         functools.partial(rank_kernel_body, tensors),
-        grid=(users,),
-        out_shape=jax.ShapeDtypeStruct((users, 1, items), F32),
+        grid=(users // step,),
+        out_shape=jax.ShapeDtypeStruct((users // step, step, items), F32),
         in_specs=[
-            pl.BlockSpec((1, items, width), lambda u: (u, 0, 0)),
-            full3, full3, own, own,
-            pl.BlockSpec((1, tensors, cols), lambda u: (u, 0, 0)),
-            pl.BlockSpec((1, tensors, cols), lambda u: (u, 0, 0)),
-            pl.BlockSpec((1, 1, cols), lambda u: (u, 0, 0)),
-            pl.BlockSpec((1, 1, cols), lambda u: (u, 0, 0)),
+            pl.BlockSpec((step, items, width), lambda u: (u, 0, 0)),
+            full, full, own, own,
+            pl.BlockSpec((step, tensors, cols), lambda u: (u, 0, 0)),
+            pl.BlockSpec((step, tensors, cols), lambda u: (u, 0, 0)),
+            pl.BlockSpec((step, 1, cols), lambda u: (u, 0, 0)),
+            pl.BlockSpec((step, 1, cols), lambda u: (u, 0, 0)),
             pl.BlockSpec(cross.shape, lambda u: (0, 0)),
             line, line,
         ],
-        out_specs=pl.BlockSpec((1, 1, items), lambda u: (u, 0, 0)),
-        compiler_params=pltpu.CompilerParams(vmem_limit_bytes=40 << 20),
+        out_specs=pl.BlockSpec((1, step, items), lambda u: (u, 0, 0)),
+        compiler_params=pltpu.CompilerParams(vmem_limit_bytes=48 << 20),
     )(rows, proj_all, first_all, proj, first, base0, base1, own0, own1, cross, bias, weight)
 
 
@@ -206,11 +230,12 @@
     two = 2 * width
     cols = proj_in.shape[1]
 
+    user_count = lax.axis_size("user")
+    share = width // user_count
     proj_here = proj_in[two:]
-    proj_all = lax.all_gather(proj_here, "tensor", axis=0)
-    flat_proj = jnp.moveaxis(proj_all, 0, 1).reshape(width, tensors * cols)
-    first_here = jnp.dot(flat_proj, cross_w[0], preferred_element_type=F32).astype(BF16)
-    first_all = lax.all_gather(first_here, "tensor", axis=0)
+    proj_piece = lax.dynamic_slice(
+        proj_here, (lax.axis_index("user") * share, 0), (share, cols)
+    )
 
     requests = users * beam
     cap_b = max(2, -(-requests // owners))
@@ -228,7 +253,12 @@
     lists = jnp.concatenate([n_list, i_list], axis=1)
     lanes = -(-lists.shape[1] // 128) * 128
     lists = jnp.pad(lists, ((0, 0), (0, lanes - lists.shape[1])))[:, None, :]
-    (asked,) = exchange(0, True, ("peer", lists))
+    asked, proj_wide = exchange(0, ("peer", lists), ("tensor", proj_piece))
+    first_piece = jnp.dot(
+        jnp.moveaxis(proj_wide, 0, 1).reshape(share, tensors * cols),
+        cross_w[0],
+        preferred_element_type=F32,
+    ).astype(BF16)
     n_asked = asked[:, 0, :cap_b].reshape(-1)
     i_asked = asked[:, 0, cap_b : cap_b + cap_i].reshape(-1)
 
@@ -250,8 +280,13 @@
     )
     back_lanes = -(-cap_b // 128) * 128
     back = jnp.pad(scores.reshape(owners, cap_b), ((0, 0), (0, back_lanes - cap_b)))[:, None, :]
-    sums, scored, arrived = exchange(
-        1, True, ("all", numerator), ("peer", back), ("leaf", sent)
+    sums, scored, first_wide, proj_all, arrived = exchange(
+        1,
+        ("all", numerator),
+        ("peer", back),
+        ("tensor", first_piece),
+        ("user", proj_wide),
+        ("leaf", sent),
     )
     interest = jnp.sum(sums, axis=0) / math.sqrt(owners * beam)
     own_scores = scored[:, 0, :cap_b]
@@ -261,11 +296,11 @@
 
     shared = jnp.concatenate([user_feat, interest.astype(BF16)], axis=1)
     own0 = jnp.dot(shared, proj_in[:two], preferred_element_type=F32)
-    (all0,) = exchange(2, False, ("all", own0))
+    all0, first_all = exchange(2, ("tensor", own0), ("user", first_wide))
     base0 = jnp.moveaxis(all0, 0, 1)
     flat0 = base0.reshape(users, tensors * cols).astype(BF16)
     own1 = jnp.dot(flat0, cross_w[0], preferred_element_type=F32) + cross_b[0]
-    (all1,) = exchange(3, False, ("all", own1))
+    (all1,) = exchange(3, ("tensor", own1))
     base1 = jnp.moveaxis(all1, 0, 1)
 
     run_marks = i_owner[:, None, :] == jnp.arange(owners, dtype=jnp.int32)[None, :, None]
@@ -278,12 +313,15 @@
         preferred_element_type=F32,
     ).astype(BF16).reshape(users, items, width)
 
+    first_here = lax.dynamic_slice(
+        first_all, (0, tensor_at, 0, 0), (user_count, 1, share, cols)
+    ).reshape(width, cols)
     partial = rank_rows(
         item_rows, proj_all, first_all, proj_here, first_here, base0, base1,
         own0[:, None, :], own1[:, None, :], cross_w[1], cross_b[1][None, :],
         out_w.astype(F32)[None, :],
     )
-    (parts,) = exchange(4, False, ("all", partial.reshape(users, items)))
+    (parts,) = exchange(4, ("tensor", partial.reshape(users, items)))
     logit = jnp.sum(parts, axis=0)
     return (beam_score, interest, logit)
 

time: 106 us -> 74 us (0.70)
  blocking collectives: 31 us -> 0 us
  Pallas kernels: 55.8 us -> 53.6 us
    all_gather x2 -> x0, blocking collectives: 31 us -> none  [the longest x1 15.7 us: per_device(): first_all = lax.all_gather(first_here, 'tensor', axis=0)]
    pallas_call x6, Pallas kernels: 55.8 us -> 53.6 us  [the longest x5 45 us: exchange(): pl.pallas_call(functools.partial(exchange_kernel, modes, sizes), out_shap...]
where the time goes in v3:
time: 74 us; the launch traced here: 73.5 us
  Pallas kernels  53.6 us (72%)
  matrix products  8.41 us (11%)
  local copies, waits for them, and re-layouts  6.23 us (8%)
  other arithmetic  4.22 us (6%)
  between operations  1 us (1%)
    pallas_call x5, Pallas kernels, exchange(): pl.pallas_call(functools.partial(exchange_kernel, modes, sizes), out_shap...  45 us
    pallas_call x1, Pallas kernels, rank_rows(): pl.pallas_call(functools.partial(rank_kernel_body, tensors), grid=(users...  8.6 us
    dot_general x1, matrix products, per_device(): jnp.dot(jnp.moveaxis(proj_wide, 0, 1).reshape(share, tensors * cols), cro...  2.09 us
    dot_general x2, matrix products, pick_rows(): return jnp.dot(hot, table, preferred_element_type=F32).astype(BF16)  2.09 us
    dot_general x1, matrix products, per_device(): own1 = jnp.dot(flat0, cross_w[0], preferred_element_type=F32) + cross_b[0]  1.96 us
    reshape x2, local copies, waits for them, and re-layouts, per_device(): item_ids.reshape(-1)  1.54 us
    reduce_sum x2, other arithmetic, small_lookup(): return jnp.sum(jnp.where(hits, table, 0), axis=-1)  1.5 us

profile of v3, /device:TPU:0, one launch (start us, length us, event | category | flops | bytes accessed | tf_op | source)
XLA Modules:
  0.0 73.5 jit_solution(15447727597863418303)
XLA Ops:
  0.6 0.0 copy-start
  0.6 0.0 copy-start.4
  0.7 0.0 copy-start.3
  0.7 0.8 %reshape.281 = s32[128]{0:T(128)S(1)} reshape(s32[8,16]{1,0:T(8,128)} %param.15) | data formatting | bytes 1024 | tf_op jit(solution)/shard_map/reshape | solution.py:242
  1.5 0.7 %select_reduce_fusion.4 = s32[128]{0:T(128)S(1)} fusion(s32[32]{0:T(128)} %param.17, s32[128]{0:T(128)S(1)} %and_select_fusion.7), kind=kLoop, calls=%fused_computation.61 | loop fusion | flops 12160 | bytes 1152 | tf_op jit(solution)/shard_map/reduce_sum | solution.py:20
  2.3 0.7 broadcast_in_dim.131
  3.0 0.1 convolution_convert_fusion.4
  3.1 0.2 select_reduce_fusion.3
  3.3 0.7 reshape.294
  4.0 0.8 %fusion.61 = (f32[1,512]{1,0:T(1,128)S(1)}, f32[1,512]{1,0:T(1,128)S(1)}) fusion(f32[2,512]{1,0:T(2,128)} %param.26), kind=kLoop, calls=%fused_computation.132 | loop fusion | bytes 8192 | tf_op jit(solution)/shard_map/slice | solution.py:321
  4.8 0.8 %reshape.283 = s32[4,384]{1,0:T(4,128)S(1)} reshape(s32[8,192]{1,0:T(8,128)} %param.16) | data formatting | bytes 12288 | tf_op jit(solution)/shard_map/reshape | solution.py:248
  5.6 0.8 %reshape.282 = s32[1536]{0:T(1024)S(1)} reshape(s32[8,192]{1,0:T(8,128)} %param.16) | data formatting | bytes 12288 | tf_op jit(solution)/shard_map/reshape | solution.py:248
  6.4 0.8 %select_reduce_fusion.1 = s32[1536]{0:T(1024)S(1)} fusion(s32[32]{0:T(128)} %param.17, s32[1536]{0:T(1024)S(1)} %add_select_fusion), kind=kLoop, calls=%fused_computation.40 | loop fusion | flops 145920 | bytes 12416 | tf_op jit(solution)/shard_map/reduce_sum | solution.py:20
  7.2 0.2 fusion.18
  7.4 0.1 convolution_convert_fusion.3
  7.5 0.3 select_reduce_fusion
  7.8 0.0 copy-start.5
  7.8 0.0 copy-start.6
  7.9 0.1 pad_add_fusion
  7.9 0.9 %slice.28.own_proj = bf16[128,512]{1,0:T(8,128)(2,1)S(1)} slice(bf16[384,512]{1,0:T(8,128)(2,1)} %param.24), slice={[256:384], [0:512]} | slice | bytes 262144 | tf_op jit(solution)/shard_map/slice | solution.py:235
  8.9 9.8 %shard_map.157 = (s32[8,1,128]{2,1,0:T(1,128)S(1)}, bf16[4,32,512]{2,1,0:T(8,128)(2,1)S(1)}) custom-call(s32[8,1,128]{2,1,0:T(1,128)S(1)} %bitcast.64, bf16[32,512]{1,0:T(8,128)(2,1)S(1)} %constant_dynamic-slice_fusion.1.refs_1_), custom_call_target="tpu_custom_call" | custom-call | tf_op jit(solution)/shard_map/pallas_call | solution.py:132
  18.7 0.1 slice_reduce_fusion
  18.8 0.1 eq.187
  18.9 0.1 reshape_squeeze.3
  19.0 1.4 %convolution_convert_fusion.1 = bf16[128,128]{1,0:T(8,128)(2,1)S(1)} fusion(bf16[2048,128]{1,0:T(8,128)(2,1)} %param.18, s32[128]{0:T(128)S(1)} %get-tuple-element.29), kind=kOutput, calls=%fused_computation.20 | convolution fusion | flops 67387392 | bytes 557568 | tf_op jit(solution)/shard_map/dot_general | solution.py:38
  20.4 0.0 copy-done
  20.4 0.7 fusion.12
  21.1 0.0 copy-start.2
  21.1 2.1 %fusion.13.refs_2_ = bf16[32,512]{1,0:T(8,128)(2,1)S(1)} fusion(bf16[32,2048]{1,0:T(8,128)(2,1)S(1)} %bitcast.70, bf16[2,2048,512]{2,1,0:T(8,128)(2,1)} %param.25), kind=kOutput, calls=%fused_computation.17 | convolution fusion | flops 67125248 | bytes 2260992 | tf_op jit(solution)/shard_map/dot_general | solution.py:257
  23.2 0.0 copy-done.4
  23.3 0.0 copy-done.3
  23.3 0.4 fusion.17
  23.6 0.0 copy-done.5
  23.7 0.0 copy-done.6
  23.7 0.4 add_divide_fusion
  24.0 0.4 fusion.30.refs_0_
  24.4 0.1 reshape.284
  24.5 16.5 %shard_map.158 = (f32[8,8,128]{2,1,0:T(8,128)S(1)}, f32[8,1,128]{2,1,0:T(1,128)S(1)}, bf16[4,32,512]{2,1,0:T(8,128)(2,1)S(1)}, bf16[4,4,32,512]{3,2,1,0:T(8,128)(2,1)S(1)}, bf16[8,192,128]{2,1,0:T(8,128)(2,1)S(1)}) custom-call(f32[8,128]{1,0:T(8,128)S(1)} %fusion.30.refs_0_, f32[8,1,128]{2,1,0:T(1,128)S(1)} %bitcast.63, bf16[32,512]{1,0:T(8,128)(2,1)S(1)} %fusion.13.refs_2_, ...), custom_call_target="tpu_custom_call" | custom-call | tf_op jit(solution)/shard_map/pallas_call | solution.py:132
  41.0 0.1 select_reduce_fusion.2
  41.1 0.7 reshape.287
  41.8 0.0 copy-start.1
  41.8 0.6 fusion.60
  42.4 0.0 copy-done.2
  42.4 0.1 fusion.26.refs_0_
  42.6 0.6 fusion.9
  43.2 7.4 %shard_map.159 = (f32[4,8,512]{2,1,0:T(8,128)S(1)}, bf16[4,4,32,512]{3,2,1,0:T(8,128)(2,1)S(1)}) custom-call(f32[8,512]{1,0:T(8,128)S(1)} %fusion.26.refs_0_, bf16[4,32,512]{2,1,0:T(8,128)(2,1)S(1)} %get-tuple-element.18.refs_1_), custom_call_target="tpu_custom_call" | custom-call | tf_op jit(solution)/shard_map/pallas_call | solution.py:132
  50.8 2.0 %fusion.19.refs_0_ = f32[8,512]{1,0:T(8,128)S(1)} fusion(bf16[8,2048]{1,0:T(8,128)(2,1)S(1)} %bitcast.68, bf16[2,2048,512]{2,1,0:T(8,128)(2,1)} %param.25, f32[512]{0:T(512)S(1)} %bitcast.71), kind=kOutput, calls=%fused_computation.24 | convolution fusion | flops 16781312 | bytes 2148352 | tf_op jit(solution)/shard_map/dot_general | solution.py:302
  52.7 5.7 %shard_map.160 = f32[4,8,512]{2,1,0:T(8,128)S(1)} custom-call(f32[8,512]{1,0:T(8,128)S(1)} %fusion.19.refs_0_), custom_call_target="tpu_custom_call" | custom-call | tf_op jit(solution)/shard_map/pallas_call | solution.py:132
  58.5 0.0 copy-done.1
  58.5 0.1 slice_bitcast_fusion.cross
  58.7 8.6 %shard_map.161 = f32[2,4,192]{2,1,0:T(4,128)S(1)} custom-call(bf16[8,192,128]{2,1,0:T(8,128)(2,1)S(1)} %bitcast.58, bf16[4,4,32,512]{3,2,1,0:T(8,128)(2,1)S(1)} %get-tuple-element.17.proj_ref, bf16[4,4,32,512]{3,2,1,0:T(8,128)(2,1)S(1)} %get-tuple-element.19.first_ref, bf16[128,512]{1,0:T(8,128)(2,1)S(1)} %slice.28.own_proj, bf16[128,512]{1,0:T(8,128)(2,1)S(1)} %bitcast.56, ...), custom_call_target="tpu_custom_call" | custom-call | tf_op jit(solution)/shard_map/pallas_call | solution.py:179
  67.3 5.6 %shard_map.162 = f32[4,8,192]{2,1,0:T(8,128)S(1)} custom-call(f32[8,192]{1,0:T(8,128)S(1)} %reshape.292.refs_0_), custom_call_target="tpu_custom_call" | custom-call | tf_op jit(solution)/shard_map/pallas_call | solution.py:132
  72.9 0.6 reduce_sum.82
  (30 shorter events, 0.5 us)
Async XLA Ops:
  0.6 19.8 %copy-start = (bf16[2048,128]{1,0:T(8,128)(2,1)S(1)}, bf16[2048,128]{1,0:T(8,128)(2,1)}, u32[]{:S(2)}) copy-start(bf16[2048,128]{1,0:T(8,128)(2,1)} %param.19) | copy-start | bytes 1572868
  0.6 22.6 %copy-start.4 = (bf16[8,128]{1,0:T(8,128)(2,1)S(1)}, bf16[8,128]{1,0:T(8,128)(2,1)}, u32[]{:S(2)}) copy-start(bf16[8,128]{1,0:T(8,128)(2,1)} %param.14) | copy-start | bytes 6148
  0.7 22.6 %copy-start.3 = (bf16[128,1024]{1,0:T(8,128)(2,1)S(1)}, bf16[128,1024]{1,0:T(8,128)(2,1)}, u32[]{:S(2)}) copy-start(bf16[128,1024]{1,0:T(8,128)(2,1)} %param.20) | copy-start | bytes 786436
  7.8 15.8 %copy-start.5 = (bf16[128,1024]{1,0:T(8,128)(2,1)S(1)}, bf16[128,1024]{1,0:T(8,128)(2,1)}, u32[]{:S(2)}) copy-start(bf16[128,1024]{1,0:T(8,128)(2,1)} %param.21) | copy-start | bytes 786436
  7.8 15.8 %copy-start.6 = (f32[1024]{0:T(1024)S(1)}, f32[1024]{0:T(1024)}, u32[]{:S(2)}) copy-start(f32[1024]{0:T(1024)} %param.22) | copy-start | bytes 12292
  21.1 21.3 %copy-start.2 = (bf16[384,512]{1,0:T(8,128)(2,1)S(1)}, bf16[384,512]{1,0:T(8,128)(2,1)}, u32[]{:S(2)}) copy-start(bf16[384,512]{1,0:T(8,128)(2,1)} %param.24) | copy-start | bytes 1179652
  41.8 16.7 %copy-start.1 = (bf16[2,2048,512]{2,1,0:T(8,128)(2,1)S(1)}, bf16[2,2048,512]{2,1,0:T(8,128)(2,1)}, u32[]{:S(2)}) copy-start(bf16[2,2048,512]{2,1,0:T(8,128)(2,1)} %param.25) | copy-start | bytes 12582916

commit v4 on v3

--- a/solution.py
+++ b/solution.py
@@ -142,57 +142,117 @@
 
 
 def rank_kernel_body(
-    tensors, rows_ref, proj_ref, first_ref, own_proj, own_first, base0, base1, own0, own1,
-    cross, bias, weight, out_ref,
+    sizes, rows_ref, proj_ref, first_wide, own_proj, own0, cross, bias, weight, out_ref,
+    first_ref, all0, all1, own1, part, parts,
+    first_send, first_recv, send0, recv0, send1, recv1, send2, recv2,
 ):
+    tensors, user_count = sizes
+    tensor, user = lax.axis_index("tensor"), lax.axis_index("user")
     users, items, width = rows_ref.shape
-    rows = rows_ref[...].reshape(users * items, width)
     cols = own_proj.shape[1]
+    extent = {"tensor": tensors, "user": user_count}
+    index = {"tensor": tensor, "user": user}
+
+    def each(axis, body):
+        pl.loop(1, extent[axis])(body)
+
+    def target(axis, k):
+        return {axis: (index[axis] + k) % extent[axis]}
+
+    def copy(axis, src, out, sends, recvs, k):
+        return pltpu.make_async_remote_copy(
+            src_ref=src,
+            dst_ref=out.at[index[axis]],
+            send_sem=sends.at[k - 1],
+            recv_sem=recvs.at[k - 1],
+            device_id=target(axis, k),
+            device_id_type=pl.DeviceIdType.MESH,
+        )
+
+    def begin(*what):
+        each(what[0], lambda k: copy(*what, k).start())
+        what[2][index[what[0]]] = what[1][...]
+
+    def finish(*what):
+        each(what[0], lambda k: copy(*what, k).wait())
 
     def dot(left, right):
         return jnp.dot(left, right, preferred_element_type=F32)
 
-    def layer(proj, first, add0, add1):
-        x0 = dot(rows, proj).reshape(users, items, cols) + add0
-        return x0, x0 * (dot(rows, first).reshape(users, items, cols) + add1) + x0
-
-    second = jnp.zeros((users * items, cols), F32)
+    barrier = pltpu.get_barrier_semaphore()
+    for axis in extent:
+        each(
+            axis,
+            lambda k: pl.semaphore_signal(
+                barrier, inc=1, device_id=target(axis, k), device_id_type=pl.DeviceIdType.MESH
+            ),
+        )
+    pl.semaphore_wait(barrier, tensors + user_count - 2)
+
+    shares = ("tensor", own0, all0, send0, recv0)
+    products = ("tensor", own1, all1, send1, recv1)
+    weights = ("user", first_wide, first_ref, first_send, first_recv)
+    logits = ("tensor", part, parts, send2, recv2)
+    begin(*shares)
+    begin(*weights)
+    finish(*shares)
+    total = bias[0:1]
     for t in range(tensors):
-        proj = proj_ref[:, t].reshape(width, cols)
-        first = first_ref[:, t].reshape(width, cols)
-        _, x1 = layer(proj, first, base0[:, t : t + 1], base1[:, t : t + 1])
-        x1 = x1.astype(BF16).reshape(users * items, cols)
-        second += dot(x1, cross[t * cols : (t + 1) * cols, :])
-    x0, x1 = layer(own_proj[...], own_first[...], own0[...], own1[...])
-    x2 = x0 * (second.reshape(users, items, cols) + bias[...]) + x1
-    out_ref[0] = jnp.sum(x2 * weight[...], axis=2)
-
-
-def rank_rows(rows, proj_all, first_all, proj, first, base0, base1, own0, own1, cross, bias, weight):
+        total = total + dot(all0[t].astype(BF16), cross[0, t * cols : (t + 1) * cols, :])
+    own1[...] = total
+    begin(*products)
+    finish(*weights)
+    finish(*products)
+
+    def layer(rows, proj, first, add0, add1):
+        count = add0.shape[0]
+        x0 = dot(rows, proj).reshape(count, items, cols) + add0[:, None, :]
+        return x0, x0 * (dot(rows, first).reshape(count, items, cols) + add1[:, None, :]) + x0
+
+    step = math.gcd(users, 4)
+    for u in range(0, users, step):
+        held = slice(u, u + step)
+        rows = rows_ref[held].reshape(step * items, width)
+        second = jnp.zeros((step * items, cols), F32)
+        for t in range(tensors):
+            proj = proj_ref[:, t].reshape(width, cols)
+            first = first_ref[:, t].reshape(width, cols)
+            _, x1 = layer(rows, proj, first, all0[t, held], all1[t, held])
+            x1 = x1.astype(BF16).reshape(step * items, cols)
+            second += dot(x1, cross[1, t * cols : (t + 1) * cols, :])
+        own_first = first_ref[:, tensor].reshape(width, cols)
+        x0, x1 = layer(rows, own_proj[...], own_first, own0[held], own1[held])
+        x2 = x0 * (second.reshape(step, items, cols) + bias[1:2]) + x1
+        part[held] = jnp.sum(x2 * weight[...], axis=2)
+    begin(*logits)
+    finish(*logits)
+    out_ref[...] = jnp.sum(parts[...], axis=0)
+
+
+def rank_rows(collective_id, rows, proj_all, first_wide, own_proj, own0, cross, bias, weight):
     users, items, width = rows.shape
-    tensors = proj_all.shape[1]
-    cols = proj.shape[1]
-    step = math.gcd(users, 4)
-    full = pl.BlockSpec(proj_all.shape, lambda u: (0, 0, 0, 0))
-    own = pl.BlockSpec((width, cols), lambda u: (0, 0))
-    line = pl.BlockSpec((1, cols), lambda u: (0, 0))
+    user_count, tensors = proj_all.shape[:2]
+    cols = own_proj.shape[1]
+    vmem = pl.BlockSpec(memory_space=pltpu.VMEM)
     return pl.pallas_call(
-        functools.partial(rank_kernel_body, tensors),
-        grid=(users // step,),
-        out_shape=jax.ShapeDtypeStruct((users // step, step, items), F32),
-        in_specs=[
-            pl.BlockSpec((step, items, width), lambda u: (u, 0, 0)),
-            full, full, own, own,
-            pl.BlockSpec((step, tensors, cols), lambda u: (u, 0, 0)),
-            pl.BlockSpec((step, tensors, cols), lambda u: (u, 0, 0)),
-            pl.BlockSpec((step, 1, cols), lambda u: (u, 0, 0)),
-            pl.BlockSpec((step, 1, cols), lambda u: (u, 0, 0)),
-            pl.BlockSpec(cross.shape, lambda u: (0, 0)),
-            line, line,
-        ],
-        out_specs=pl.BlockSpec((1, step, items), lambda u: (u, 0, 0)),
-        compiler_params=pltpu.CompilerParams(vmem_limit_bytes=48 << 20),
-    )(rows, proj_all, first_all, proj, first, base0, base1, own0, own1, cross, bias, weight)
+        functools.partial(rank_kernel_body, (tensors, user_count)),
+        out_shape=jax.ShapeDtypeStruct((users, items), F32),
+        in_specs=[vmem] * 8,
+        out_specs=vmem,
+        scratch_shapes=[
+            pltpu.VMEM(proj_all.shape, BF16),
+            pltpu.VMEM((tensors, users, cols), F32),
+            pltpu.VMEM((tensors, users, cols), F32),
+            pltpu.VMEM((users, cols), F32),
+            pltpu.VMEM((users, items), F32),
+            pltpu.VMEM((tensors, users, items), F32),
+        ]
+        + [pltpu.SemaphoreType.DMA((user_count - 1,))] * 2
+        + [pltpu.SemaphoreType.DMA((tensors - 1,))] * 6,
+        compiler_params=pltpu.CompilerParams(
+            collective_id=collective_id, has_side_effects=True, vmem_limit_bytes=48 << 20
+        ),
+    )(rows, proj_all, first_wide, own_proj, own0, cross, bias, weight)
 
 
 def request_lists(owner, coded, owners, cap):
@@ -296,13 +356,6 @@
 
     shared = jnp.concatenate([user_feat, interest.astype(BF16)], axis=1)
     own0 = jnp.dot(shared, proj_in[:two], preferred_element_type=F32)
-    all0, first_all = exchange(2, ("tensor", own0), ("user", first_wide))
-    base0 = jnp.moveaxis(all0, 0, 1)
-    flat0 = base0.reshape(users, tensors * cols).astype(BF16)
-    own1 = jnp.dot(flat0, cross_w[0], preferred_element_type=F32) + cross_b[0]
-    (all1,) = exchange(3, ("tensor", own1))
-    base1 = jnp.moveaxis(all1, 0, 1)
-
     run_marks = i_owner[:, None, :] == jnp.arange(owners, dtype=jnp.int32)[None, :, None]
     run_rank = jnp.sum(jnp.where(run_marks, rank_in_row(run_marks), 0), axis=1)
     place = run_rank + i_owner * cap_i
@@ -313,16 +366,10 @@
         preferred_element_type=F32,
     ).astype(BF16).reshape(users, items, width)
 
-    first_here = lax.dynamic_slice(
-        first_all, (0, tensor_at, 0, 0), (user_count, 1, share, cols)
-    ).reshape(width, cols)
-    partial = rank_rows(
-        item_rows, proj_all, first_all, proj_here, first_here, base0, base1,
-        own0[:, None, :], own1[:, None, :], cross_w[1], cross_b[1][None, :],
+    logit = rank_rows(
+        2, item_rows, proj_all, first_wide, proj_here, own0, cross_w, cross_b,
         out_w.astype(F32)[None, :],
     )
-    (parts,) = exchange(4, ("tensor", partial.reshape(users, items)))
-    logit = jnp.sum(parts, axis=0)
     return (beam_score, interest, logit)
 
 

time: 74 us -> 68.7 us (0.928)
  Pallas kernels: 53.6 us -> 48.2 us
  local copies, waits for them, and re-layouts: 6.23 us -> 7.91 us
  other arithmetic: 4.22 us -> 3 us
    pallas_call x5 -> x2, Pallas kernels: 45 us -> 26.3 us  [exchange(): pl.pallas_call(functools.partial(exchange_kernel, modes, sizes), out_shap...]
    pallas_call x1, Pallas kernels: 8.6 us -> 21.8 us  [rank_rows(): pl.pallas_call(functools.partial(rank_kernel_body, (tensors, user_count))...]
    unnamed x16 -> x14, local copies, waits for them, and re-layouts: 0.74 us -> 3.51 us
    dot_general x1 -> x0, matrix products: 1.96 us -> none  [per_device(): own1 = jnp.dot(flat0, cross_w[0], preferred_element_type=F32) + cross_b[0]]
    dot_general x1, matrix products: 0.37 us -> 1.34 us  [per_device(): jnp.dot(user_rows, mlp_user, preferred_element_type=F32)]
    dot_general x1, matrix products: 0.37 us -> 1.32 us  [per_device(): scores = jnp.dot(hidden, mlp_out, preferred_element_type=F32)]
    slice x1 -> x0, local copies, waits for them, and re-layouts: 0.77 us -> none  [per_device(): cross_b[1][None, :]]
where the time goes in v4:
time: 68.7 us; the launch traced here: 68.2 us
  Pallas kernels  48.2 us (70%)
  matrix products  8.28 us (12%)
  local copies, waits for them, and re-layouts  7.91 us (12%)
  other arithmetic  3 us (4%)
  between operations  0.88 us (1%)
    pallas_call x2, Pallas kernels, exchange(): pl.pallas_call(functools.partial(exchange_kernel, modes, sizes), out_shap...  26.3 us
    pallas_call x1, Pallas kernels, rank_rows(): pl.pallas_call(functools.partial(rank_kernel_body, (tensors, user_count))...  21.8 us
    unnamed x14, local copies, waits for them, and re-layouts  3.51 us
    dot_general x2, matrix products, pick_rows(): return jnp.dot(hot, table, preferred_element_type=F32).astype(BF16)  2.09 us
    dot_general x1, matrix products, per_device(): jnp.dot(jnp.moveaxis(proj_wide, 0, 1).reshape(share, tensors * cols), cro...  2.08 us
    reshape x2, local copies, waits for them, and re-layouts, per_device(): item_ids.reshape(-1)  1.6 us
    reduce_sum x2, other arithmetic, small_lookup(): return jnp.sum(jnp.where(hits, table, 0), axis=-1)  1.5 us

profile of v4, /device:TPU:0, one launch (start us, length us, event | category | flops | bytes accessed | tf_op | source)
XLA Modules:
  0.0 68.2 jit_solution(4724317675707633016)
XLA Ops:
  0.6 0.0 copy-start
  0.6 0.8 %reshape.275 = s32[4,384]{1,0:T(4,128)S(1)} reshape(s32[8,192]{1,0:T(8,128)} %param.16) | data formatting | bytes 12288 | tf_op jit(solution)/shard_map/reshape | solution.py:308
  1.5 0.8 %reshape.274 = s32[1536]{0:T(1024)S(1)} reshape(s32[8,192]{1,0:T(8,128)} %param.16) | data formatting | bytes 12288 | tf_op jit(solution)/shard_map/reshape | solution.py:308
  2.3 0.8 %select_reduce_fusion.1 = s32[1536]{0:T(1024)S(1)} fusion(s32[32]{0:T(128)} %param.17, s32[1536]{0:T(1024)S(1)} %add_select_fusion), kind=kLoop, calls=%fused_computation.35 | loop fusion | flops 145920 | bytes 12416 | tf_op jit(solution)/shard_map/reduce_sum | solution.py:20
  3.1 0.1 convolution_convert_fusion.3
  3.3 0.2 select_reduce_fusion
  3.5 0.8 %reshape.273 = s32[128]{0:T(128)S(1)} reshape(s32[8,16]{1,0:T(8,128)} %param.15) | data formatting | bytes 1024 | tf_op jit(solution)/shard_map/reshape | solution.py:302
  4.3 0.7 %select_reduce_fusion.4 = s32[128]{0:T(128)S(1)} fusion(s32[32]{0:T(128)} %param.17, s32[128]{0:T(128)S(1)} %and_select_fusion.7), kind=kLoop, calls=%fused_computation.53 | loop fusion | flops 12160 | bytes 1152 | tf_op jit(solution)/shard_map/reduce_sum | solution.py:20
  5.1 0.1 convolution_convert_fusion.4
  5.2 0.2 select_reduce_fusion.3
  5.5 0.1 pad_add_fusion
  5.5 0.9 %slice.18.own_proj = bf16[128,512]{1,0:T(8,128)(2,1)S(1)} slice(bf16[384,512]{1,0:T(8,128)(2,1)} %param.24), slice={[256:384], [0:512]} | slice | bytes 262144 | tf_op jit(solution)/shard_map/slice | solution.py:295
  6.5 9.8 %shard_map.157 = (s32[8,1,128]{2,1,0:T(1,128)S(1)}, bf16[4,32,512]{2,1,0:T(8,128)(2,1)S(1)}) custom-call(s32[8,1,128]{2,1,0:T(1,128)S(1)} %bitcast.39, bf16[32,512]{1,0:T(8,128)(2,1)S(1)} %constant_dynamic-slice_fusion.refs_1_), custom_call_target="tpu_custom_call" | custom-call | tf_op jit(solution)/shard_map/pallas_call | solution.py:132
  16.3 0.1 reshape_squeeze.3
  16.4 1.4 %convolution_convert_fusion.1 = bf16[128,128]{1,0:T(8,128)(2,1)S(1)} fusion(bf16[2048,128]{1,0:T(8,128)(2,1)} %param.18, s32[128]{0:T(128)S(1)} %get-tuple-element.23), kind=kOutput, calls=%fused_computation.16 | convolution fusion | flops 67387392 | bytes 557568 | tf_op jit(solution)/shard_map/dot_general | solution.py:38
  17.8 0.7 %reshape.284 = bf16[1024,1]{0,1:T(2,128)(2,1)S(1)} reshape(bf16[1024]{0:T(1024)(128)(2,1)} %param.23) | data formatting | bytes 4096 | tf_op args[9]
  18.5 1.3 %fusion.14 = f32[128,1024]{1,0:T(8,128)S(1)} fusion(bf16[128,1024]{1,0:T(8,128)(2,1)} %param.20, bf16[8,128]{1,0:T(8,128)(2,1)} %param.14, s32[128]{0:T(128)S(1)} %get-tuple-element.22), kind=kOutput, calls=%fused_computation.18 | convolution fusion | flops 33833984 | bytes 788992 | tf_op jit(solution)/shard_map/dot_general | solution.py:331
  19.9 1.3 %add_divide_fusion = (f32[128]{0:T(128)S(1)}, f32[128]{0:T(128)S(1)}) fusion(bf16[1024,1]{0,1:T(2,128)(2,1)S(1)} %reshape.284, f32[128,1024]{1,0:T(8,128)S(1)} %fusion.14, bf16[128,128]{1,0:T(8,128)(2,1)S(1)} %convolution_convert_fusion.1, bf16[128,1024]{1,0:T(8,128)(2,1)} %param.21, f32[1024]{0:T(1024)} %param.22), kind=kOutput, calls=%fused_computation.115 | convolution fusion | flops 34734464 | bytes 826368 | tf_op jit(solution)/shard_map/dot_general | solution.py:336
  21.2 0.1 broadcast_compare_fusion.2
  21.3 0.3 fusion.24.refs_0_
  21.6 0.1 reshape.276
  21.7 0.0 copy-start.3
  21.7 0.0 copy-start.4
  21.7 0.0 copy-start.5
  21.7 0.0 copy-start.2
  21.7 2.1 %fusion.10.refs_2_ = bf16[32,512]{1,0:T(8,128)(2,1)S(1)} fusion(bf16[32,2048]{1,0:T(8,128)(2,1)S(1)} %bitcast.43, bf16[2,2048,512]{2,1,0:T(8,128)(2,1)} %cross.1), kind=kOutput, calls=%fused_computation.13 | convolution fusion | flops 67125248 | bytes 2260992 | tf_op jit(solution)/shard_map/dot_general | solution.py:317
  23.8 0.1 slice_reduce_fusion
  23.9 0.1 eq.187
  24.0 0.0 copy-done
  24.0 0.7 %fusion.9 = bf16[384,128]{1,0:T(8,128)(2,1)S(1)} fusion(bf16[2048,128]{1,0:T(8,128)(2,1)S(1)} %copy-done, s32[384]{0:T(512)S(1)} %eq.187), kind=kOutput, calls=%fused_computation.12 | convolution fusion | flops 202162176 | bytes 624128 | tf_op jit(solution)/shard_map/dot_general | solution.py:38
  24.7 16.5 %shard_map.158 = (f32[8,8,128]{2,1,0:T(8,128)S(1)}, f32[8,1,128]{2,1,0:T(1,128)S(1)}, bf16[4,32,512]{2,1,0:T(8,128)(2,1)S(1)}, bf16[4,4,32,512]{3,2,1,0:T(8,128)(2,1)S(1)}, bf16[8,192,128]{2,1,0:T(8,128)(2,1)S(1)}) custom-call(f32[8,128]{1,0:T(8,128)S(1)} %fusion.24.refs_0_, f32[8,1,128]{2,1,0:T(1,128)S(1)} %bitcast.38, bf16[32,512]{1,0:T(8,128)(2,1)S(1)} %fusion.10.refs_2_, ...), custom_call_target="tpu_custom_call" | custom-call | tf_op jit(solution)/shard_map/pallas_call | solution.py:132
  41.2 0.1 select_reduce_fusion.2
  41.3 0.7 reshape.279
  42.0 0.6 fusion.53
  42.6 0.2 fusion.15
  42.9 0.6 fusion.6
  43.4 0.0 copy-done.3
  43.4 0.0 copy-done.4
  43.4 0.1 fusion.20.own0
  43.6 0.0 copy-done.5
  43.6 0.0 copy-done.2
  43.6 0.0 copy-start.1
  43.6 2.2 %copy-done.1 = bf16[2,2048,512]{2,1,0:T(8,128)(2,1)S(1)} copy-done((bf16[2,2048,512]{2,1,0:T(8,128)(2,1)S(1)}, bf16[2,2048,512]{2,1,0:T(8,128)(2,1)}, u32[]{:S(2)}) %copy-start.1) | copy-done | bytes 4194328
  45.8 21.8 %shard_map.159 = f32[8,192]{1,0:T(8,128)S(1)} custom-call(bf16[8,192,128]{2,1,0:T(8,128)(2,1)S(1)} %bitcast.35, bf16[4,4,32,512]{3,2,1,0:T(8,128)(2,1)S(1)} %get-tuple-element.15.proj_ref, bf16[4,32,512]{2,1,0:T(8,128)(2,1)S(1)} %get-tuple-element.16.first_wide, bf16[128,512]{1,0:T(8,128)(2,1)S(1)} %slice.18.own_proj, f32[8,512]{1,0:T(8,128)S(1)} %fusion.20.own0, ...), custom_call_target="tpu_custom_call" | custom-call | tf_op jit(solution)/shard_map/pallas_call | solution.py:237
  67.6 0.6 copy.24
  (22 shorter events, 0.3 us)
Async XLA Ops:
  0.6 23.4 %copy-start = (bf16[2048,128]{1,0:T(8,128)(2,1)S(1)}, bf16[2048,128]{1,0:T(8,128)(2,1)}, u32[]{:S(2)}) copy-start(bf16[2048,128]{1,0:T(8,128)(2,1)} %param.19) | copy-start | bytes 1572868
  21.7 21.7 %copy-start.3 = (bf16[384,512]{1,0:T(8,128)(2,1)S(1)}, bf16[384,512]{1,0:T(8,128)(2,1)}, u32[]{:S(2)}) copy-start(bf16[384,512]{1,0:T(8,128)(2,1)} %param.24) | copy-start | bytes 1179652
  21.7 21.7 %copy-start.4 = (bf16[8,128]{1,0:T(8,128)(2,1)S(1)}, bf16[8,128]{1,0:T(8,128)(2,1)}, u32[]{:S(2)}) copy-start(bf16[8,128]{1,0:T(8,128)(2,1)} %param.14) | copy-start | bytes 6148
  21.7 21.9 %copy-start.5 = (bf16[512]{0:T(512)(128)(2,1)S(1)}, bf16[512]{0:T(512)(128)(2,1)}, u32[]{:S(2)}) copy-start(bf16[512]{0:T(512)(128)(2,1)} %param.27) | copy-start | bytes 3076
  21.7 21.9 %copy-start.2 = (f32[2,512]{1,0:T(2,128)S(1)}, f32[2,512]{1,0:T(2,128)}, u32[]{:S(2)}) copy-start(f32[2,512]{1,0:T(2,128)} %bias.1) | copy-start | bytes 12292
  43.6 2.2 %copy-start.1 = (bf16[2,2048,512]{2,1,0:T(8,128)(2,1)S(1)}, bf16[2,2048,512]{2,1,0:T(8,128)(2,1)}, u32[]{:S(2)}) copy-start(bf16[2,2048,512]{2,1,0:T(8,128)(2,1)} %cross.1) | copy-start | bytes 12582916
